TPU v7x, 128 devices: a whole 4x4x4 slice. The times are simulated.
128 devices in a mesh: req: 16 (over y_hi, x, core), head: 8 (over y_lo, z).
Axes of the slice: x: 4, y: 4 (y_hi: 2, y_lo: 2; y = y_hi * 2 + y_lo), z: 4, core: 2. Of those that a mesh axis runs over, the one named last changes fastest.
Arguments:
- hidden: bfloat16 [512, 16, 2048], P('req', None, 'head'), may hold values from -6 to 6
- w_zx: bfloat16 [2048, 2, 4096], P(None, None, 'head'), may hold values from -0.125 to 0.125
- w_bc: bfloat16 [2048, 256], replicated, may hold values from -0.125 to 0.125
- w_dt: bfloat16 [2048, 64], P(None, 'head'), may hold values from -0.125 to 0.125
- conv_x_w: float32 [5, 4096], P(None, 'head'), may hold values from -3 to 3
- conv_bc_w: float32 [5, 256], replicated, may hold values from -3 to 3
- dt_bias: float32 [64], P('head'), may hold values from -4 to 0.5
- a_log: float32 [64], P('head'), may hold values from 0 to 2.5
- d_skip: float32 [64], P('head'), may hold values from 0.5 to 1.5
- norm_gain: float32 [4096], P('head'), may hold values from 0.1 to 1.9
- w_out: bfloat16 [4096, 2048], P('head'), may hold values from -0.09375 to 0.09375
- ssm_state: float32 [512, 64, 64, 128], P('req', 'head'), may hold values from -3 to 3
- conv_x_state: float32 [512, 3, 4096], P('req', None, 'head'), may hold values from -6 to 6
- conv_bc_state: float32 [512, 3, 256], P('req'), may hold values from -6 to 6
- slot: int32 [512], replicated, may hold values from 0 to 511, as said below
- lengths: int32 [512], replicated, may hold values from 0 to 16
- accepted: int32 [512], replicated, may hold values from 0 to 16
Outputs:
- out: bfloat16 [512, 16, 2048], P('req', None, 'head')
- new_state: float32 [512, 64, 64, 128], P('req', 'head')
- new_conv_x: float32 [512, 3, 4096], P('req', None, 'head')
- new_conv_bc: float32 [512, 3, 256], P('req')
Inputs may be any that keep to these rules, and one draw needn't show every extreme that they name: slot is a permutation of the pool rows; the requests of each aligned block of 32 requests have exactly 2 pool rows in each aligned block of 32 pool rows.
All inputs are finite; a program needn't handle non-finite values.
Results may differ from a plain program's by a relative error of at most 0.0082.
Values may be sent and summed in bfloat16 or wider, within the bound.
No kernel may reach another device: no remote copies, remote signals or barrier semaphores. Data moves between devices by JAX's collectives and lax.ppermute only.
A program may use at most 128 MiB of HBM per device.

v0:
```python
import jax
import jax.numpy as jnp
from jax import lax
from jax.sharding import PartitionSpec as P

highest = lax.Precision.HIGHEST


def conv_step(previous, inputs, taps):
    window = jnp.concatenate([previous, inputs.astype(jnp.float32)], axis=1)
    tail = taps.shape[0] - 1
    steps = inputs.shape[1]
    total = taps[tail] + taps[0] * window[:, 0:steps]
    for tap in range(1, tail):
        total = total + taps[tap] * window[:, tap : tap + steps]
    return (jax.nn.silu(total).astype(jnp.bfloat16), window)


def keep_rows(window, counted, tail):
    picks = counted[:, None] + jnp.arange(tail, dtype=jnp.int32)[None, :]
    return jnp.take_along_axis(window, picks[:, :, None], axis=1)


def scan_block(x_conv, bc_conv, dt_in, states, counted, dt_bias, a_log, d_skip):
    heads = states.shape[1]
    nstate = states.shape[3]
    blocks, steps, chans = x_conv.shape
    headdim = chans // heads
    xh = x_conv.astype(jnp.float32).reshape(blocks, steps, heads, headdim)
    bmat = bc_conv[..., :nstate].astype(jnp.float32)
    cmat = bc_conv[..., nstate:].astype(jnp.float32)
    step_size = jax.nn.softplus(dt_in.astype(jnp.float32) + dt_bias)
    rate = step_size * -jnp.exp(a_log)
    cumul = jnp.cumsum(rate, axis=1)
    carried = jnp.exp(cumul)[..., None] * jnp.einsum(
        "bhpn,btn->bthp", states, cmat, precision=highest
    )
    inner = jnp.einsum("btn,bsn->bts", cmat, bmat, precision=highest)
    places = jnp.arange(steps, dtype=jnp.int32)
    lower = (places[:, None] >= places[None, :])[None, :, :, None]
    spread = cumul[:, :, None, :] - cumul[:, None, :, :]
    factor = jnp.where(lower, jnp.exp(jnp.where(lower, spread, 0.0)), 0.0)
    factor = factor * inner[..., None] * step_size[:, None, :, :]
    within = jnp.einsum("btsh,bshp->bthp", factor, xh, precision=highest)
    mixed = (
        (carried + within + d_skip[:, None] * xh).reshape(blocks, steps, chans).astype(jnp.bfloat16)
    )
    live = (places[None, :] < counted[:, None])[..., None]
    total = jnp.sum(jnp.where(live, rate, 0.0), axis=1)
    remain = jnp.where(live, total[:, None, :] - cumul, 0.0)
    scaled = jnp.where(live, jnp.exp(remain) * step_size, 0.0)
    updated = jnp.exp(total)[:, :, None, None] * states
    updated = updated + jnp.einsum("bsh,bshp,bsn->bhpn", scaled, xh, bmat, precision=highest)
    return (mixed, updated)


def advance(
    x_pre,
    bc_pre,
    dt_pre,
    conv_x_prev,
    conv_bc_prev,
    states,
    counted,
    conv_x_w,
    conv_bc_w,
    dt_bias,
    a_log,
    d_skip,
):
    tail = conv_x_prev.shape[1]
    x_conv, x_window = conv_step(conv_x_prev, x_pre, conv_x_w)
    bc_conv, bc_window = conv_step(conv_bc_prev, bc_pre, conv_bc_w)
    mixed, updated = scan_block(x_conv, bc_conv, dt_pre, states, counted, dt_bias, a_log, d_skip)
    return (mixed, updated, keep_rows(x_window, counted, tail), keep_rows(bc_window, counted, tail))


def per_device(
    hidden,
    w_zx,
    w_bc,
    w_dt,
    conv_x_w,
    conv_bc_w,
    dt_bias,
    a_log,
    d_skip,
    norm_gain,
    w_out,
    ssm_state,
    conv_x_state,
    conv_bc_state,
    slot,
    lengths,
    accepted,
):
    local_requests, steps, width_part = hidden.shape
    width = w_zx.shape[0]
    local_inner = w_zx.shape[2]
    bc_cols = w_bc.shape[1]
    stacked = jnp.concatenate([w_zx.reshape(width, 2 * local_inner), w_bc, w_dt], axis=1)
    piece = lax.all_gather(hidden, "head", axis=2, tiled=True)
    projected = jnp.dot(
        piece.reshape(-1, piece.shape[2]), stacked, preferred_element_type=jnp.float32
    )
    projected = projected.astype(jnp.bfloat16).reshape(local_requests, steps, -1)
    gate_in = projected[..., :local_inner]
    x_in = projected[..., local_inner : 2 * local_inner]
    bc_in = projected[..., 2 * local_inner : 2 * local_inner + bc_cols]
    dt_in = projected[..., 2 * local_inner + bc_cols :]
    myself = lax.axis_index("req")
    peers = lax.axis_size("req")
    per_peer = local_requests // peers
    slot_blocks = slot.reshape(peers, local_requests)
    owner_blocks = slot_blocks // local_requests
    local_rows = slot_blocks % local_requests
    by_owner = jnp.argsort(owner_blocks, axis=1, stable=True)
    my_order = lax.dynamic_index_in_dim(by_owner, myself, 0, keepdims=False)
    undo_order = jnp.argsort(my_order)
    selected = lax.dynamic_slice_in_dim(by_owner, myself * per_peer, per_peer, 1)
    arrive_rows = jnp.take_along_axis(local_rows, selected, axis=1).reshape(local_requests)
    to_pool = jnp.argsort(arrive_rows)
    counted = jnp.minimum(accepted, lengths)
    counted_blocks = counted.reshape(peers, local_requests)
    my_lengths = lax.dynamic_index_in_dim(
        lengths.reshape(peers, local_requests), myself, 0, keepdims=False
    )
    outgoing = (
        jnp.take(ssm_state, arrive_rows, axis=0),
        jnp.take(conv_x_state, arrive_rows, axis=0),
        jnp.take(conv_bc_state, arrive_rows, axis=0),
    )
    states_in, conv_x_in, conv_bc_in = (
        lax.all_to_all(outgoing[0], "req", split_axis=0, concat_axis=0, tiled=True),
        lax.all_to_all(outgoing[1], "req", split_axis=0, concat_axis=0, tiled=True),
        lax.all_to_all(outgoing[2], "req", split_axis=0, concat_axis=0, tiled=True),
    )
    my_counted = jnp.take(
        lax.dynamic_index_in_dim(counted_blocks, myself, 0, keepdims=False), my_order, axis=0
    )
    mixed_sorted, states_out, conv_x_out, conv_bc_out = advance(
        jnp.take(x_in, my_order, axis=0),
        jnp.take(bc_in, my_order, axis=0),
        jnp.take(dt_in, my_order, axis=0),
        conv_x_in,
        conv_bc_in,
        states_in,
        my_counted,
        conv_x_w,
        conv_bc_w,
        dt_bias,
        a_log,
        d_skip,
    )
    mixed = jnp.take(mixed_sorted, undo_order, axis=0)
    back_states, back_conv_x, back_conv_bc = (
        lax.all_to_all(states_out, "req", split_axis=0, concat_axis=0, tiled=True),
        lax.all_to_all(conv_x_out, "req", split_axis=0, concat_axis=0, tiled=True),
        lax.all_to_all(conv_bc_out, "req", split_axis=0, concat_axis=0, tiled=True),
    )
    new_state = jnp.take(back_states, to_pool, axis=0)
    new_conv_x = jnp.take(back_conv_x, to_pool, axis=0)
    new_conv_bc = jnp.take(back_conv_bc, to_pool, axis=0)
    gated = mixed.astype(jnp.float32) * jax.nn.silu(gate_in.astype(jnp.float32))
    squares = lax.psum(jnp.sum(gated * gated, axis=-1), "head")
    meansq = squares / (local_inner * lax.axis_size("head"))
    normed = (gated * lax.rsqrt(meansq + 1e-05)[..., None] * norm_gain).astype(jnp.bfloat16)
    partial_out = jnp.dot(
        normed.reshape(-1, local_inner), w_out, preferred_element_type=jnp.float32
    ).reshape(local_requests, steps, width)
    summed = lax.psum_scatter(partial_out, "head", scatter_dimension=2, tiled=True)
    places = jnp.arange(steps, dtype=jnp.int32)
    valid = places[None, :] < my_lengths[:, None]
    out = jnp.where(valid[..., None], summed, 0.0).astype(jnp.bfloat16)
    return (out, new_state, new_conv_x, new_conv_bc)


def solution(mesh):
    in_specs = (
        P("req", None, "head"),
        P(None, None, "head"),
        P(),
        P(None, "head"),
        P(None, "head"),
        P(),
        P("head"),
        P("head"),
        P("head"),
        P("head"),
        P("head", None),
        P("req", "head", None, None),
        P("req", None, "head"),
        P("req", None, None),
        P(),
        P(),
        P(),
    )
    out_specs = (
        P("req", None, "head"),
        P("req", "head", None, None),
        P("req", None, "head"),
        P("req", None, None),
    )
    return jax.shard_map(
        per_device, mesh=mesh, in_specs=in_specs, out_specs=out_specs, check_vma=False
    )
```

profile of v0, /device:TPU:1, one launch (start us, length us, event | category | flops | bytes accessed | tf_op | source)
XLA Modules:
  0.0 478.6 jit_solution(8611803134680669130)
XLA Ops:
  15.7 8.4 %all-to-all-start = ((f32[32,3,256]{2,1,0:T(4,128)}), f32[32,3,256]{2,1,0:T(4,128)S(1)}, u32[]{:S(2)}, u32[]{:S(2)}) async-start(f32[32,3,256]{2,1,0:T(4,128)} %copy_select_fusion), calls=%async_computation | async-start | bytes 262144 | tf_op jit(solution)/shard_map/all_to_all | solution.py:136
  25.9 7.9 %gather_fusion.7 = f32[32,8,64,128]{3,2,1,0:T(8,128)} fusion(f32[32,8,64,128]{3,2,1,0:T(8,128)} %param.36, s32[1024]{0:T(1024)S(1)} %pad_clamp_fusion.3), kind=kCustom, calls=%fused_computation.1.clone | custom fusion | bytes 16777344 | tf_op jit(solution)/shard_map/jit(_take)/gather | solution.py:129
  34.4 7.2 %all-to-all-start.2 = ((f32[32,3,512]{2,1,0:T(4,128)}), f32[32,3,512]{2,1,0:T(4,128)S(1)}, u32[]{:S(2)}, u32[]{:S(2)}) async-start(f32[32,3,512]{2,1,0:T(4,128)} %copy.86), calls=%async_computation.2 | async-start | bytes 524288 | tf_op jit(solution)/shard_map/all_to_all | solution.py:135
  41.6 8.8 %broadcast_select_fusion.1 = f32[32,8,64,128]{3,2,1,0:T(8,128)} fusion(f32[32,8,64,128]{3,2,1,0:T(8,128)} %gather_fusion.7, pred[32]{0:T(512)(128)(4,1)S(1)} %get-tuple-element.47), kind=kLoop, calls=%fused_computation.22 | loop fusion | flops 2097152 | bytes 16777248 | tf_op jit(solution)/shard_map/jit(_take)/select_n | solution.py:129
  51.2 7.2 %all-to-all-start.1 = ((f32[32,8,64,128]{3,2,1,0:T(8,128)}), f32[32,8,64,128]{3,2,1,0:T(8,128)}, u32[]{:S(2)}, u32[]{:S(2)}) async-start(f32[32,8,64,128]{3,2,1,0:T(8,128)} %broadcast_select_fusion.1), calls=%async_computation.1 | async-start | bytes 16777216 | tf_op jit(solution)/shard_map/all_to_all | solution.py:134
  59.7 5.4 %copy.101 = bf16[256,8,2,512]{3,1,2,0:T(8,128)(2,1)} copy(bf16[256,8,2,512]{3,2,1,0:T(2,128)(2,1)} %bitcast.56) | data formatting | bytes 8388608
  68.7 104.9 %all-gather.2.cloned.1.call-done = bf16[32,16,2048]{2,1,0:T(8,128)(2,1)} async-done(((bf16[32,16,256]{2,1,0:T(8,128)(2,1)}), bf16[32,16,2048]{2,1,0:T(8,128)(2,1)}) %all-gather.2.cloned.1.call-update) | async-done | bytes 2097168 | tf_op jit(solution)/shard_map/all_gather | solution.py:102
  173.6 7.6 %fusion.9 = bf16[512,1288]{0,1:T(8,128)(2,1)} fusion(bf16[512,2048]{1,0:T(8,128)(2,1)} %bitcast.68, bf16[2048,8]{1,0:T(8,128)(2,1)S(1)} %copy.77, bf16[2048,256]{1,0:T(8,128)(2,1)} %param.27, bf16[2048,1024]{1,0:T(8,128)(2,1)} %bitcast.57), kind=kOutput, calls=%fused_computation.28 | convolution fusion | flops 2717618176 | bytes 8691712 | tf_op jit(solution)/shard_map/dot_general | solution.py:103
  181.2 2.0 copy.78
  187.2 2.2 gather_fusion
  193.5 2.4 gather_fusion.1
  199.8 2.1 gather_fusion.5
  202.7 2.6 gather_fusion.9
  208.5 2.9 gather_fusion.4
  213.2 2.4 multiply_convert_fusion.1
  217.2 2.1 multiply_select_fusion
  226.6 2.4 multiply_convert_fusion.3
  231.0 2.9 fusion.16
  233.9 13.3 %all-to-all-start.5 = ((f32[32,3,256]{2,1,0:T(4,128)}), f32[32,3,256]{2,1,0:T(4,128)}, u32[]{:S(2)}, u32[]{:S(2)}) async-start(f32[32,3,256]{2,1,0:T(4,128)} %broadcast_select_fusion.6), calls=%async_computation.6 | async-start | bytes 262144 | tf_op jit(solution)/shard_map/all_to_all | solution.py:159
  247.2 13.9 %fusion.13 = bf16[32,16,8,64]{3,1,2,0:T(8,128)(2,1)S(1)} fusion(f32[32,8,64,16]{2,3,1,0:T(8,128)} %fusion.16, f32[32,8,64,128]{3,2,1,0:T(8,128)} %all-to-all-done.1, f32[8]{0:T(128)S(1)} %copy-done.25, f32[32,16,8]{1,2,0:T(8,128)} %copy.81, bf16[32,16,8,64]{3,2,1,0:T(8,128)(2,1)S(1)} %reshape.281, bf16[32,16,256]{2,1,0:T(8,128)(2,1)S(1)} %multiply_convert_fusion.3), kind=kOutput, calls=%fused_computation.32 | convolution fusion | flops 404226048 | bytes 11158016 | tf_op jit(solution)/shard_map/bhpn,btn->bthp/dot_general | solution.py:35
  262.3 2.6 convert_element_type.54
  264.9 2.6 gather_fusion.10
  267.5 13.1 %multiply_add_fusion = f32[32,8,64,128]{3,2,1,0:T(8,128)} fusion(f32[32,8,64,128]{3,2,1,0:T(8,128)} %all-to-all-done.1, f32[32,8]{1,0:T(8,128)S(1)} %copy-done.14, f32[32,16,8]{1,2,0:T(8,128)S(1)} %copy.93, bf16[32,16,8,64]{3,2,1,0:T(8,128)(2,1)S(1)} %reshape.281, bf16[32,16,256]{2,1,0:T(8,128)(2,1)S(1)} %multiply_convert_fusion.3), kind=kOutput, calls=%fused_computation.14 | convolution fusion | flops 407371776 | bytes 18104320 | tf_op jit(solution)/shard_map/bsh,bshp,bsn->bhpn/dot_general | solution.py:53
  282.1 26.2 %psum.7 = f32[32,16]{1,0:T(8,128)S(1)} all-reduce(f32[32,16]{1,0:T(8,128)S(1)} %multiply_reduce_fusion), channel_id=1, replica_groups=mesh['req'=16,'head'=8] {'head'}, use_global_device_ids=true, to_apply=%region_4.9 | all-reduce | flops 512 | bytes 4096 | tf_op jit(solution)/shard_map/psum | solution.py:165
  308.4 15.1 %all-to-all-start.4 = ((f32[32,3,512]{2,1,0:T(4,128)}), f32[32,3,512]{2,1,0:T(4,128)S(1)}, u32[]{:S(2)}, u32[]{:S(2)}) async-start(f32[32,3,512]{2,1,0:T(4,128)} %broadcast_select_fusion.3), calls=%async_computation.5 | async-start | bytes 524288 | tf_op jit(solution)/shard_map/all_to_all | solution.py:158
  323.5 8.6 %all-to-all-done.4 = f32[32,3,512]{2,1,0:T(4,128)S(1)} async-done(((f32[32,3,512]{2,1,0:T(4,128)}), f32[32,3,512]{2,1,0:T(4,128)S(1)}, u32[]{:S(2)}, u32[]{:S(2)}) %all-to-all-start.4) | async-done | bytes 196640 | tf_op jit(solution)/shard_map/all_to_all | solution.py:158
  332.1 5.3 %all-to-all-start.3 = ((f32[32,8,64,128]{3,2,1,0:T(8,128)}), f32[32,8,64,128]{3,2,1,0:T(8,128)}, u32[]{:S(2)}, u32[]{:S(2)}) async-start(f32[32,8,64,128]{3,2,1,0:T(8,128)} %multiply_add_fusion), calls=%async_computation.4 | async-start | bytes 16777216 | tf_op jit(solution)/shard_map/all_to_all | solution.py:157
  337.5 4.6 fusion.14
  348.4 103.6 %all-to-all-done.3 = f32[32,8,64,128]{3,2,1,0:T(8,128)} async-done(((f32[32,8,64,128]{3,2,1,0:T(8,128)}), f32[32,8,64,128]{3,2,1,0:T(8,128)}, u32[]{:S(2)}, u32[]{:S(2)}) %all-to-all-start.3) | async-done | bytes 8388640 | tf_op jit(solution)/shard_map/all_to_all | solution.py:157
  452.1 8.0 %gather_fusion.11 = f32[32,8,64,128]{3,2,1,0:T(8,128)} fusion(f32[32,8,64,128]{3,2,1,0:T(8,128)} %all-to-all-done.3, s32[1024]{0:T(1024)S(1)} %pad_clamp_fusion), kind=kCustom, calls=%fused_computation.5.clone | custom fusion | bytes 16777344 | tf_op jit(solution)/shard_map/jit(_take)/gather | solution.py:161
  460.0 8.9 %broadcast_select_fusion = f32[32,8,64,128]{3,2,1,0:T(8,128)} fusion(f32[32,8,64,128]{3,2,1,0:T(8,128)} %gather_fusion.11, pred[32]{0:T(512)(128)(4,1)S(1)} %compare_and_fusion), kind=kLoop, calls=%fused_computation.21 | loop fusion | flops 2097152 | bytes 16777248 | tf_op jit(solution)/shard_map/jit(_take)/select_n | solution.py:161
  469.5 1.9 select_convert_fusion.1
  (148 shorter events, 54.7 us)
Async XLA Ops:
  7.2 330.3 %copy-start = (bf16[512,2048]{1,0:T(8,128)(2,1)S(1)}, bf16[512,2048]{1,0:T(8,128)(2,1)}, u32[]{:S(2)}) copy-start(bf16[512,2048]{1,0:T(8,128)(2,1)} %param.35) | copy-start | bytes 6291460
  11.6 1.3 copy-start.17
  11.8 2.4 copy-start.2
  12.5 11.6 %copy-start.1 = (f32[32,3,512]{2,0,1:T(8,128)S(1)}, f32[32,3,512]{2,0,1:T(8,128)}, u32[]{:S(2)}) copy-start(f32[32,3,512]{2,0,1:T(8,128)} %param.37) | copy-start | bytes 589828
  12.9 1.3 copy-start.19
  15.7 18.1 %all-to-all-start = ((f32[32,3,256]{2,1,0:T(4,128)}), f32[32,3,256]{2,1,0:T(4,128)S(1)}, u32[]{:S(2)}, u32[]{:S(2)}) async-start(f32[32,3,256]{2,1,0:T(4,128)} %copy_select_fusion), calls=%async_computation | async-start | bytes 262144 | tf_op jit(solution)/shard_map/all_to_all | solution.py:136
  34.4 16.1 %all-to-all-start.2 = ((f32[32,3,512]{2,1,0:T(4,128)}), f32[32,3,512]{2,1,0:T(4,128)S(1)}, u32[]{:S(2)}, u32[]{:S(2)}) async-start(f32[32,3,512]{2,1,0:T(4,128)} %copy.86), calls=%async_computation.2 | async-start | bytes 524288 | tf_op jit(solution)/shard_map/all_to_all | solution.py:135
  50.5 8.9 %copy-start.15 = (bf16[2048,8]{0,1:T(8,128)(2,1)S(1)}, bf16[2048,8]{0,1:T(8,128)(2,1)}, u32[]{:S(2)}) copy-start(bf16[2048,8]{0,1:T(8,128)(2,1)} %param.28) | copy-start | bytes 98308
  51.2 182.6 %all-to-all-start.1 = ((f32[32,8,64,128]{3,2,1,0:T(8,128)}), f32[32,8,64,128]{3,2,1,0:T(8,128)}, u32[]{:S(2)}, u32[]{:S(2)}) async-start(f32[32,8,64,128]{3,2,1,0:T(8,128)} %broadcast_select_fusion.1), calls=%async_computation.1 | async-start | bytes 16777216 | tf_op jit(solution)/shard_map/all_to_all | solution.py:134
  58.4 115.2 %all-gather.2.cloned.1.call-start = ((), (), s32[]{:S(2)}) async-start(), calls=%async_computation.7 | async-start | bytes 2359296 | tf_op jit(solution)/shard_map/all_gather | solution.py:102
  59.7 7.2 %copy-start.27 = (f32[8]{0:T(128)S(1)}, f32[8]{0:T(128)}, u32[]{:S(2)}) copy-start(f32[8]{0:T(128)} %param.32) | copy-start | bytes 100
  59.7 7.8 %copy-start.21 = (f32[5,256]{1,0:T(8,128)S(1)}, f32[5,256]{1,0:T(8,128)}, u32[]{:S(2)}) copy-start(f32[5,256]{1,0:T(8,128)} %param.30) | copy-start | bytes 15364
  59.7 8.4 %copy-start.18 = (f32[5,512]{1,0:T(8,128)S(1)}, f32[5,512]{1,0:T(8,128)}, u32[]{:S(2)}) copy-start(f32[5,512]{1,0:T(8,128)} %param.29) | copy-start | bytes 30724
  183.2 15.6 %copy-start.3 = (bf16[512,1288]{1,0:T(8,128)(2,1)}, bf16[512,1288]{1,0:T(8,128)(2,1)S(1)}, u32[]{:S(2)}) copy-start(bf16[512,1288]{1,0:T(8,128)(2,1)S(1)} %copy.78) | copy-start | bytes 3956740
  197.0 0.8 copy-start.4
  199.8 6.6 %copy-start.6 = (f32[32,3,512]{2,1,0:T(4,128)S(1)}, f32[32,3,512]{2,1,0:T(4,128)}, u32[]{:S(2)}) copy-start(f32[32,3,512]{2,1,0:T(4,128)} %copy-done.5) | copy-start | bytes 589828
  211.4 5.8 %copy-start.7 = (bf16[32,16,8]{2,0,1:T(8,128)(2,1)S(1)}, bf16[32,16,8]{2,0,1:T(8,128)(2,1)}, u32[]{:S(2)}) copy-start(bf16[32,16,8]{2,0,1:T(8,128)(2,1)} %copy.80) | copy-start | bytes 24580
  219.3 11.6 %copy-start.24 = (pred[16,16]{1,0:T(8,128)(4,1)S(1)}, pred[16,16]{1,0:T(8,128)(4,1)}, u32[]{:S(2)}) copy-start(pred[16,16]{1,0:T(8,128)(4,1)} %iota_compare_fusion.2) | copy-start | bytes 772
  224.9 6.1 %copy-start.12 = (f32[32,16,8]{1,2,0:T(8,128)S(1)}, f32[32,16,8]{1,2,0:T(8,128)}, u32[]{:S(2)}) copy-start(f32[32,16,8]{1,2,0:T(8,128)} %copy.89) | copy-start | bytes 49156
  224.9 6.1 %copy-start.13 = (f32[32,16,8]{1,2,0:T(8,128)S(1)}, f32[32,16,8]{1,2,0:T(8,128)}, u32[]{:S(2)}) copy-start(f32[32,16,8]{1,2,0:T(8,128)} %copy.87) | copy-start | bytes 49156
  230.9 16.2 %copy-start.25 = (f32[8]{0:T(128)S(1)}, f32[8]{0:T(128)}, u32[]{:S(2)}) copy-start(f32[8]{0:T(128)} %param.33) | copy-start | bytes 100
  233.9 74.5 %all-to-all-start.5 = ((f32[32,3,256]{2,1,0:T(4,128)}), f32[32,3,256]{2,1,0:T(4,128)}, u32[]{:S(2)}, u32[]{:S(2)}) async-start(f32[32,3,256]{2,1,0:T(4,128)} %broadcast_select_fusion.6), calls=%async_computation.6 | async-start | bytes 262144 | tf_op jit(solution)/shard_map/all_to_all | solution.py:159
  261.1 6.4 %copy-start.14 = (f32[32,8]{1,0:T(8,128)S(1)}, f32[32,8]{1,0:T(8,128)}, u32[]{:S(2)}) copy-start(f32[32,8]{1,0:T(8,128)} %exp.49) | copy-start | bytes 3076
  267.5 13.1 %copy-start.8 = (bf16[32,16,512]{2,1,0:T(8,128)(2,1)S(1)}, bf16[32,16,512]{2,1,0:T(8,128)(2,1)}, u32[]{:S(2)}) copy-start(bf16[32,16,512]{2,1,0:T(8,128)(2,1)} %gather_fusion.10) | copy-start | bytes 1572868
  267.5 13.1 %copy-start.22 = (pred[32]{0:T(512)(128)(4,1)S(1)}, pred[32]{0:T(512)(128)(4,1)}, u32[]{:S(2)}) copy-start(pred[32]{0:T(512)(128)(4,1)} %get-tuple-element.46) | copy-start | bytes 100
  308.4 23.7 %all-to-all-start.4 = ((f32[32,3,512]{2,1,0:T(4,128)}), f32[32,3,512]{2,1,0:T(4,128)S(1)}, u32[]{:S(2)}, u32[]{:S(2)}) async-start(f32[32,3,512]{2,1,0:T(4,128)} %broadcast_select_fusion.3), calls=%async_computation.5 | async-start | bytes 524288 | tf_op jit(solution)/shard_map/all_to_all | solution.py:158
  323.5 14.0 %copy-start.9 = (bf16[32,16,512]{2,1,0:T(8,128)(2,1)S(1)}, bf16[32,16,512]{2,1,0:T(8,128)(2,1)}, u32[]{:S(2)}) copy-start(bf16[32,16,512]{2,1,0:T(8,128)(2,1)} %gather_fusion.10) | copy-start | bytes 1572868
  323.5 14.0 %copy-start.23 = (pred[32]{0:T(512)(128)(4,1)S(1)}, pred[32]{0:T(512)(128)(4,1)}, u32[]{:S(2)}) copy-start(pred[32]{0:T(512)(128)(4,1)} %get-tuple-element.46) | copy-start | bytes 100
  323.5 14.0 %copy-start.26 = (f32[512]{0:T(512)S(1)}, f32[512]{0:T(512)}, u32[]{:S(2)}) copy-start(f32[512]{0:T(512)} %param.34) | copy-start | bytes 6148
  332.1 119.9 %all-to-all-start.3 = ((f32[32,8,64,128]{3,2,1,0:T(8,128)}), f32[32,8,64,128]{3,2,1,0:T(8,128)}, u32[]{:S(2)}, u32[]{:S(2)}) async-start(f32[32,8,64,128]{3,2,1,0:T(8,128)} %multiply_add_fusion), calls=%async_computation.4 | async-start | bytes 16777216 | tf_op jit(solution)/shard_map/all_to_all | solution.py:157
  337.4 132.1 %reduce-scatter.2.cloned.1.call-start = ((), (), s32[]{:S(2)}) async-start(), calls=%async_computation.8 | async-start | bytes 4718592 | tf_op jit(solution)/shard_map/reduce_scatter | solution.py:171
  342.0 0.8 copy-start.20
  (4 other events, 2.7 us)
Sparse Core Ops, SparseCore 0:
  60.8 112.7 all-gather.1
  342.2 127.2 reduce-scatter.1
where the time goes:
time: 487 us; the launch traced here: 479 us
  waiting for transfers between devices  218 us (45%)
  local copies, waits for them, and re-layouts  74.9 us (15%)
  starting transfers between devices  56.6 us (12%)
  other arithmetic  45.3 us (9%)
  matrix products  42.2 us (9%)
  blocking collectives  26.2 us (5%)
  between operations  14.9 us (3%)
    all_gather x1, waiting for transfers between devices, per_device(): piece = lax.all_gather(hidden, 'head', axis=2, tiled=True)  105 us
    all_to_all x1, waiting for transfers between devices, per_device(): lax.all_to_all(states_out, 'req', split_axis=0, concat_axis=0, tiled=True)  104 us
    psum x1, blocking collectives, per_device(): squares = lax.psum(jnp.sum(gated * gated, axis=-1), 'head')  26.2 us
    all_to_all x1, starting transfers between devices, per_device(): lax.all_to_all(conv_x_out, 'req', split_axis=0, concat_axis=0, tiled=True)  15.1 us
    dot_general x1, matrix products, scan_block(): jnp.einsum('bhpn,btn->bthp', states, cmat, precision=highest)  13.9 us
    all_to_all x1, starting transfers between devices, per_device(): lax.all_to_all(conv_bc_out, 'req', split_axis=0, concat_axis=0, tiled=True)  13.3 us
    dot_general x1, matrix products, scan_block(): jnp.einsum('bsh,bshp,bsn->bhpn', scaled, xh, bmat, precision=highest)  13.1 us
    unnamed x61, local copies, waits for them, and re-layouts  12.2 us
  transfers between devices with their start and end apart: 8, of which 4 were waited for; matrix products, arithmetic and copies ran while one was open for 31% of the time, Pallas kernels for 0%

commit v1 on v0

v1 whole, which is shorter than its diff:
```python
import functools

import jax
import jax.numpy as jnp
from jax import lax
from jax.experimental import pallas as pl
from jax.experimental.pallas import tpu as pltpu
from jax.sharding import PartitionSpec as P

f32 = jnp.float32
bf16 = jnp.bfloat16
highest = lax.Precision.HIGHEST
NT = (((1,), (1,)), ((), ()))
TN = (((0,), (0,)), ((), ()))
STAT_ROWS = 8


def send_kernel(info, hid_ref, out_ref, seen, *, heads_dev):
    requests = hid_ref.shape[0]
    peers = seen.shape[0]
    for o in range(peers):
        seen[o] = 0

    def body(i, carry):
        owner = lax.div(info[i], requests)
        j = seen[owner]
        seen[owner] = j + 1
        rows = hid_ref[i]
        for h in range(heads_dev):
            out_ref[(owner * heads_dev + h) * 2 + j] = rows
        return carry

    lax.fori_loop(0, requests, body, 0)


def layer_kernel(
    arrive,
    recv_ref,
    wzx_ref,
    wbc_ref,
    wdt_ref,
    wout_ref,
    cxw_ref,
    cbw_ref,
    bias_ref,
    alog_ref,
    skip_ref,
    gain_ref,
    cvec_ref,
    cx_ref,
    cb_ref,
    state_hbm,
    out_ref,
    ncx_ref,
    ncb_ref,
    newstate_hbm,
    st_ref,
    xw_ref,
    bw_ref,
    gate_ref,
    dt_ref,
    ec_ref,
    sc_ref,
    fd_ref,
    dec_ref,
    g_ref,
    sq_ref,
    in_sem,
    out_sem,
    *,
    heads_dev,
):
    requests = cx_ref.shape[0]
    tail = cx_ref.shape[1]
    inner = xw_ref.shape[2]
    steps = recv_ref.shape[1]
    part = recv_ref.shape[2]
    peers = recv_ref.shape[0] // (2 * heads_dev)
    tokens = requests * steps
    nstate = st_ref.shape[2]
    heads = wdt_ref.shape[1]
    headdim = inner // heads
    spread = heads * steps
    base = 8 - tail
    blk = 256

    def load_state(i):
        return pltpu.make_async_copy(state_hbm.at[arrive[i]], st_ref.at[i], in_sem.at[i])

    def save_state(i):
        return pltpu.make_async_copy(st_ref.at[i], newstate_hbm.at[arrive[i]], out_sem.at[i])

    lax.fori_loop(0, requests, lambda i, c: (load_state(i).start(), c)[1], 0)

    view = recv_ref.reshape(peers, heads_dev, 2, steps, part)
    tok = jnp.concatenate(
        [view[:, h].reshape(tokens, part) for h in range(heads_dev)], axis=1
    )

    def proj(w):
        return jnp.dot(tok, w, preferred_element_type=f32).astype(bf16)

    for n in range(inner // blk):
        gate_ref[:, n * blk : (n + 1) * blk] = proj(wzx_ref[:, n * blk : (n + 1) * blk])
    for n in range(inner // blk):
        xw_ref[:, 8 : 8 + steps, n * blk : (n + 1) * blk] = (
            proj(wzx_ref[:, inner + n * blk : inner + (n + 1) * blk])
            .astype(f32)
            .reshape(requests, steps, blk)
        )
    bw_ref[:, 8 : 8 + steps, :] = proj(wbc_ref[...]).astype(f32).reshape(requests, steps, 2 * nstate)
    dt_in = proj(wdt_ref[...]).astype(f32)

    pre = dt_in + bias_ref[...]
    dt = jnp.maximum(pre, 0.0) + jnp.log1p(jnp.exp(-jnp.abs(pre)))
    rate = -dt * jnp.exp(alog_ref[...])
    place = lax.rem(lax.broadcasted_iota(jnp.int32, (tokens, heads), 0), steps)
    cumul = rate
    d = 1
    while d < steps:
        cumul = cumul + jnp.where(place >= d, pltpu.roll(cumul, d, 0), 0.0)
        d *= 2
    live = place < cvec_ref[...]
    total = jnp.sum(jnp.where(live, rate, 0.0).reshape(requests, steps, heads), axis=1, keepdims=True)
    dec_ref[...] = jnp.exp(total)
    totals = jnp.broadcast_to(total, (requests, steps, heads)).reshape(tokens, heads)
    scaled = jnp.where(live, jnp.exp(jnp.where(live, totals - cumul, 0.0)) * dt, 0.0)

    def pick(width, each):
        rows = lax.broadcasted_iota(jnp.int32, (heads, width), 0)
        cols = lax.div(lax.broadcasted_iota(jnp.int32, (heads, width), 1), each)
        return (rows == cols).astype(f32)

    to_chan = pick(inner, headdim)
    to_pair = pick(spread, steps)
    ec_ref[...] = jnp.dot(
        jnp.exp(cumul), to_chan, precision=highest, preferred_element_type=f32
    ).reshape(requests, steps, inner)
    sc_ref[...] = jnp.dot(
        scaled, to_chan, precision=highest, preferred_element_type=f32
    ).reshape(requests, steps, inner)
    cum2 = jnp.dot(cumul, to_pair, precision=highest, preferred_element_type=f32).reshape(
        requests, steps, spread
    )
    dt2 = jnp.dot(dt, to_pair, precision=highest, preferred_element_type=f32).reshape(
        requests, steps, spread
    )
    t_at = lax.broadcasted_iota(jnp.int32, (1, steps, spread), 1)
    s_at = lax.rem(lax.broadcasted_iota(jnp.int32, (1, steps, spread), 2), steps)
    same = t_at == s_at
    lower = t_at >= s_at
    crow = jnp.sum(jnp.where(same, cum2, 0.0), axis=1, keepdims=True)
    drow = jnp.sum(jnp.where(same, dt2, 0.0), axis=1, keepdims=True)
    fd_ref[...] = jnp.where(lower, jnp.exp(jnp.where(lower, cum2 - crow, 0.0)) * drow, 0.0)

    r_head = lax.div(lax.broadcasted_iota(jnp.int32, (spread, inner), 0), steps)
    c_head = lax.div(lax.broadcasted_iota(jnp.int32, (spread, inner), 1), headdim)
    diag = (r_head == c_head).astype(bf16)

    def conv(win_ref, w_ref, i):
        total_c = w_ref[tail + 1 : tail + 2, :]
        for k in range(tail + 1):
            total_c = total_c + w_ref[k : k + 1, :] * win_ref[i, base + k : base + k + steps, :]
        return (total_c * lax.logistic(total_c)).astype(bf16)

    def body(i, carry):
        row = arrive[i]
        count = arrive[requests + i]
        xw_ref[i, base:8, :] = cx_ref[row]
        bw_ref[i, base:8, :] = cb_ref[row]
        x = conv(xw_ref, cxw_ref, i)
        bc = conv(bw_ref, cbw_ref, i)
        back = 8 + steps - base - count
        ncx_ref[row] = pltpu.roll(xw_ref[i], back, 0)[:tail]
        ncb_ref[row] = pltpu.roll(bw_ref[i], back, 0)[:tail]
        b = bc[:, :nstate]
        c = bc[:, nstate:]
        load_state(i).wait()
        state = st_ref[i]
        carried = lax.dot_general(c, state.astype(bf16), NT, preferred_element_type=f32)
        many_b = jnp.concatenate([b] * heads, axis=0)
        gram = lax.dot_general(c, many_b, NT, preferred_element_type=f32)
        factor = (gram * fd_ref[i]).astype(bf16)
        many_x = jnp.concatenate([x] * heads, axis=0) * diag
        within = jnp.dot(factor, many_x, preferred_element_type=f32)
        xf = x.astype(f32)
        mixed = (carried * ec_ref[i] + within + skip_ref[...] * xf).astype(bf16)
        push = (xf * sc_ref[i]).astype(bf16)
        update = lax.dot_general(push, b, TN, preferred_element_type=f32)
        dec = dec_ref[i]
        for h in range(heads):
            sl = slice(h * headdim, (h + 1) * headdim)
            factor_h = jnp.broadcast_to(dec[:, h : h + 1], (headdim, nstate))
            st_ref[i, sl, :] = factor_h * state[sl, :] + update[sl, :]
        save_state(i).start()
        tok_at = pl.ds(pl.multiple_of(i * steps, steps), steps)
        gate = gate_ref[tok_at, :].astype(f32)
        gated = mixed.astype(f32) * (gate * lax.logistic(gate))
        sq_ref[tok_at, :] = (gated * gated).astype(bf16)
        g_ref[tok_at, :] = (gated * gain_ref[...]).astype(bf16)
        return carry

    lax.fori_loop(0, requests, body, 0)

    ones = jnp.ones((STAT_ROWS, inner), bf16)
    squares = lax.dot_general(ones, sq_ref[...], NT, preferred_element_type=f32)
    high = squares.astype(bf16).astype(f32)
    first = lax.broadcasted_iota(jnp.int32, squares.shape, 0) == 0
    stats = jnp.where(first, high, squares - high).astype(bf16)
    pair = 2 * steps
    data_rows = 2 * pair
    out_view = out_ref.reshape(peers, heads_dev, data_rows + STAT_ROWS, 128)
    for b in range(peers):
        piece = jnp.concatenate(
            [stats[:, b * pair : (b + 1) * pair], jnp.zeros((STAT_ROWS, 128 - pair), bf16)], axis=1
        )
        for h in range(heads_dev):
            out_view[b, h, data_rows:, :] = piece

    for h in range(heads_dev):
        res = jnp.dot(
            g_ref[...], wout_ref[:, h * part : (h + 1) * part], preferred_element_type=f32
        ).astype(bf16)
        out_view[:, h, 0:pair, :] = res[:, :128].reshape(peers, pair, 128)
        out_view[:, h, pair:data_rows, :] = res[:, 128:].reshape(peers, pair, 128)

    lax.fori_loop(0, requests, lambda i, c: (save_state(i).wait(), c)[1], 0)


def final_kernel(info, recv_ref, out_ref, seen, *, heads_dev, inner_all):
    requests, steps, part = out_ref.shape
    peers = seen.shape[0]
    pair = 2 * steps
    data_rows = 2 * pair
    for o in range(peers):
        seen[o] = 0
    view = recv_ref.reshape(peers, heads_dev, data_rows + STAT_ROWS, 128)
    eye = lax.broadcasted_iota(jnp.int32, (pair, 128), 0) == lax.broadcasted_iota(
        jnp.int32, (pair, 128), 1
    )
    place = lax.broadcasted_iota(jnp.int32, (steps, 128), 0)

    def body(i, carry):
        owner = lax.div(info[i], requests)
        length = info[requests + i]
        j = seen[owner]
        seen[owner] = j + 1
        stats = view[owner, 0, data_rows:, :].astype(f32)
        for h in range(1, heads_dev):
            stats = stats + view[owner, h, data_rows:, :].astype(f32)
        squares = stats[0:1, :] + stats[1:2, :]
        at = lax.broadcasted_iota(jnp.int32, (steps, 128), 0) + j * steps
        lane = lax.broadcasted_iota(jnp.int32, (steps, 128), 1)
        total = jnp.sum(jnp.where(lane == at, squares, 0.0), axis=1, keepdims=True)
        scale = lax.rsqrt(total / inner_all + 1e-05)
        keep = place < length
        for half in range(2):
            rows = pl.ds(pl.multiple_of(half * pair + j * steps, steps), steps)
            acc = view[owner, 0, rows, :].astype(f32)
            for h in range(1, heads_dev):
                acc = acc + view[owner, h, rows, :].astype(f32)
            out_ref[i, :, half * 128 : (half + 1) * 128] = jnp.where(keep, acc * scale, 0.0).astype(bf16)
        return carry

    lax.fori_loop(0, requests, body, 0)


def vmem(n):
    return [pl.BlockSpec(memory_space=pltpu.VMEM)] * n


def smem():
    return pl.BlockSpec(memory_space=pltpu.SMEM)


def any_space():
    return pl.BlockSpec(memory_space=pl.ANY)


def per_device(
    hidden,
    w_zx,
    w_bc,
    w_dt,
    conv_x_w,
    conv_bc_w,
    dt_bias,
    a_log,
    d_skip,
    norm_gain,
    w_out,
    ssm_state,
    conv_x_state,
    conv_bc_state,
    slot,
    lengths,
    accepted,
):
    requests, steps, part = hidden.shape
    width = w_zx.shape[0]
    inner = w_zx.shape[2]
    bc_cols = w_bc.shape[1]
    heads = w_dt.shape[1]
    headdim = inner // heads
    nstate = bc_cols // 2
    tail = conv_x_state.shape[1]
    peers = lax.axis_size("req")
    heads_dev = lax.axis_size("head")
    tokens = requests * steps
    spread = heads * steps
    out_rows = 4 * steps + STAT_ROWS
    me = lax.axis_index("req")

    slot_blocks = slot.reshape(peers, requests)
    mine = jnp.concatenate(
        [
            lax.dynamic_slice_in_dim(slot, me * requests, requests),
            lax.dynamic_slice_in_dim(lengths, me * requests, requests),
        ]
    )
    outgoing = pl.pallas_call(
        functools.partial(send_kernel, heads_dev=heads_dev),
        out_shape=jax.ShapeDtypeStruct((peers * heads_dev * 2, steps, part), bf16),
        in_specs=[smem()] + vmem(1),
        out_specs=vmem(1)[0],
        scratch_shapes=[pltpu.SMEM((peers,), jnp.int32)],
        name="send_rows",
    )(mine, hidden)
    arrived = lax.all_to_all(outgoing, ("req", "head"), split_axis=0, concat_axis=0, tiled=True)

    counted = jnp.minimum(accepted, lengths).reshape(peers, requests)
    order = jnp.arange(requests, dtype=jnp.int32)[None, :]
    code = (order * requests + slot_blocks % requests) * (2 * steps) + counted
    here = slot_blocks // requests == me
    low = jnp.min(jnp.where(here, code, jnp.iinfo(jnp.int32).max), axis=1)
    high = jnp.max(jnp.where(here, code, -1), axis=1)
    both = jnp.stack([low, high], axis=1).reshape(requests)
    rows = (both // (2 * steps)) % requests
    counts = both % (2 * steps)
    arrive = jnp.concatenate([rows, counts])
    count_col = jnp.broadcast_to(counts[:, None, None], (requests, steps, heads)).reshape(tokens, heads)

    leaving, new_conv_x, new_conv_bc, new_state = pl.pallas_call(
        functools.partial(layer_kernel, heads_dev=heads_dev),
        out_shape=(
            jax.ShapeDtypeStruct((peers * heads_dev, out_rows, 128), bf16),
            jax.ShapeDtypeStruct(conv_x_state.shape, f32),
            jax.ShapeDtypeStruct(conv_bc_state.shape, f32),
            jax.ShapeDtypeStruct((requests, inner, nstate), f32),
        ),
        in_specs=[smem()] + vmem(14) + [any_space()],
        out_specs=tuple(vmem(3)) + (any_space(),),
        scratch_shapes=[
            pltpu.VMEM((requests, inner, nstate), f32),
            pltpu.VMEM((requests, 8 + steps, inner), f32),
            pltpu.VMEM((requests, 8 + steps, bc_cols), f32),
            pltpu.VMEM((tokens, inner), bf16),
            pltpu.VMEM((tokens, heads), f32),
            pltpu.VMEM((requests, steps, inner), f32),
            pltpu.VMEM((requests, steps, inner), f32),
            pltpu.VMEM((requests, steps, spread), f32),
            pltpu.VMEM((requests, 1, heads), f32),
            pltpu.VMEM((tokens, inner), bf16),
            pltpu.VMEM((tokens, inner), bf16),
            pltpu.SemaphoreType.DMA((requests,)),
            pltpu.SemaphoreType.DMA((requests,)),
        ],
        compiler_params=pltpu.CompilerParams(vmem_limit_bytes=48 * 1024 * 1024),
        name="layer",
    )(
        arrive,
        arrived,
        w_zx.reshape(width, 2 * inner),
        w_bc,
        w_dt,
        w_out,
        conv_x_w,
        conv_bc_w,
        dt_bias[None, :],
        a_log[None, :],
        jnp.repeat(d_skip, headdim)[None, :],
        norm_gain[None, :],
        count_col,
        conv_x_state,
        conv_bc_state,
        ssm_state.reshape(requests, inner, nstate),
    )
    returned = lax.all_to_all(leaving, ("req", "head"), split_axis=0, concat_axis=0, tiled=True)
    out = pl.pallas_call(
        functools.partial(final_kernel, heads_dev=heads_dev, inner_all=inner * heads_dev),
        out_shape=jax.ShapeDtypeStruct((requests, steps, part), bf16),
        in_specs=[smem()] + vmem(1),
        out_specs=vmem(1)[0],
        scratch_shapes=[pltpu.SMEM((peers,), jnp.int32)],
        name="place_rows",
    )(mine, returned)
    return (out, new_state.reshape(ssm_state.shape), new_conv_x, new_conv_bc)


def solution(mesh):
    in_specs = (
        P("req", None, "head"),
        P(None, None, "head"),
        P(),
        P(None, "head"),
        P(None, "head"),
        P(),
        P("head"),
        P("head"),
        P("head"),
        P("head"),
        P("head", None),
        P("req", "head", None, None),
        P("req", None, "head"),
        P("req", None, None),
        P(),
        P(),
        P(),
    )
    out_specs = (
        P("req", None, "head"),
        P("req", "head", None, None),
        P("req", None, "head"),
        P("req", None, None),
    )
    return jax.shard_map(
        per_device, mesh=mesh, in_specs=in_specs, out_specs=out_specs, check_vma=False
    )
```

time: 487 us -> 118 us (0.24); the launches traced: 479 us -> 117 us
  waiting for transfers between devices: 218 us -> 55 us
  local copies, waits for them, and re-layouts: 74.9 us -> 12.2 us
  other arithmetic: 45.3 us -> 0.91 us
  matrix products: 42.2 us -> 0 us
  starting transfers between devices: 56.6 us -> 16.1 us
  Pallas kernels: 0 us -> 32.1 us
  blocking collectives: 26.2 us -> 0 us
  between operations: 14.9 us -> 0.87 us
    all_gather x1 -> x0, waiting for transfers between devices: 105 us -> none  [per_device(): piece = lax.all_gather(hidden, 'head', axis=2, tiled=True)]
    all_to_all x6 -> x2, waiting for transfers between devices: 112 us -> 55 us  [the longest x1 31.7 us: per_device(): lax.all_to_all(leaving, ('req', 'head'), split_axis=0, concat_axis=0, til...]
    dot_general x6 -> x0, matrix products: 42.2 us -> none  [the longest x1 13.9 us: scan_block(): jnp.einsum('bhpn,btn->bthp', states, cmat, precision=highest)]
    gather x22 -> x0, local copies, waits for them, and re-layouts: 40.4 us -> none  [the longest x1 7.96 us: per_device(): new_state = jnp.take(back_states, to_pool, axis=0)]
    all_to_all x6 -> x2, starting transfers between devices: 56.5 us -> 16.1 us  [the longest x1 11.5 us: per_device(): lax.all_to_all(outgoing, ('req', 'head'), split_axis=0, concat_axis=0, ti...]
    pallas_call x0 -> x3, Pallas kernels: none -> 32.1 us  [the longest x1 23.7 us: per_device(): pl.pallas_call(functools.partial(layer_kernel, heads_dev=heads_dev), out_...]
    psum x1 -> x0, blocking collectives: 26.2 us -> none  [per_device(): squares = lax.psum(jnp.sum(gated * gated, axis=-1), 'head')]
    select_n x14 -> x1, other arithmetic: 22.4 us -> 0.02 us  [per_device(): rows = both // (2 * steps) % requests]
  transfers between devices with their start and end apart: 8 -> 2, of which waited for: 4 -> 2; matrix products, arithmetic and copies ran while one was open for 31% -> 7% of each run, Pallas kernels for 0% -> 0%
where the time goes in v1:
time: 118 us; the launch traced here: 117 us
  waiting for transfers between devices  55 us (47%)
  Pallas kernels  32.1 us (27%)
  starting transfers between devices  16.1 us (14%)
  local copies, waits for them, and re-layouts  12.2 us (10%)
    all_to_all x1, waiting for transfers between devices, per_device(): lax.all_to_all(leaving, ('req', 'head'), split_axis=0, concat_axis=0, til...  31.7 us
    pallas_call x1, Pallas kernels, per_device(): pl.pallas_call(functools.partial(layer_kernel, heads_dev=heads_dev), out_...  23.7 us
    all_to_all x1, waiting for transfers between devices, per_device(): lax.all_to_all(outgoing, ('req', 'head'), split_axis=0, concat_axis=0, ti...  23.3 us
    all_to_all x1, starting transfers between devices, per_device(): lax.all_to_all(outgoing, ('req', 'head'), split_axis=0, concat_axis=0, ti...  11.5 us
    unnamed x34, local copies, waits for them, and re-layouts  9.96 us
    pallas_call x1, Pallas kernels, per_device(): pl.pallas_call(functools.partial(final_kernel, heads_dev=heads_dev, inner...  5.63 us
    all_to_all x1, starting transfers between devices, per_device(): lax.all_to_all(leaving, ('req', 'head'), split_axis=0, concat_axis=0, til...  4.62 us
    pallas_call x1, Pallas kernels, per_device(): pl.pallas_call(functools.partial(send_kernel, heads_dev=heads_dev), out_s...  2.76 us
  transfers between devices with their start and end apart: 2, of which 2 were waited for; matrix products, arithmetic and copies ran while one was open for 7% of the time, Pallas kernels for 0%

profile of v1, /device:TPU:1, one launch (start us, length us, event | category | flops | bytes accessed | tf_op | source)
XLA Modules:
  0.0 117.2 jit_solution(5403330598204210609)
XLA Ops:
  0.6 0.8 dynamic_slice.6
  1.4 0.8 dynamic_slice.7
  2.1 0.7 pad_add_fusion.1.info
  2.8 2.8 %send_rows.1 = bf16[256,16,256]{2,1,0:T(8,128)(2,1)} custom-call(s32[64]{0:T(128)} %pad_add_fusion.1.info, bf16[32,16,256]{2,1,0:T(8,128)(2,1)} %hid_ref.1), custom_call_target="tpu_custom_call" | custom-call | tf_op jit(solution)/shard_map/send_rows/pallas_call | solution.py:321
  5.6 0.0 copy-start.8
  5.6 11.5 %all-to-all-start = ((bf16[256,16,256]{2,1,0:T(8,128)(2,1)}), bf16[256,16,256]{2,1,0:T(8,128)(2,1)S(1)}, u32[]{:S(2)}, u32[]{:S(2)}) async-start(bf16[256,16,256]{2,1,0:T(8,128)(2,1)} %send_rows.1), calls=%async_computation | async-start | bytes 4194304 | tf_op jit(solution)/shard_map/all_to_all | solution.py:329
  17.1 0.1 reshape.54
  17.2 0.1 broadcast_in_dim.31
  17.3 0.1 broadcast_in_dim_reshape.3.skip_ref
  17.4 0.1 reshape.55
  17.5 0.1 select_reduce_fusion.1
  17.6 0.1 copy.33
  17.7 0.1 reshape.56
  17.8 0.1 broadcast_in_dim.33
  17.9 0.1 broadcast_in_dim.34
  18.0 0.1 copy.36.cb_ref
  18.1 0.1 copy.35.cx_ref
  18.2 0.3 copy.34.wdt_ref
  18.5 0.0 copy-start.2
  18.5 0.0 copy-start.3
  18.6 5.4 %copy.39 = bf16[256,8,2,512]{3,1,2,0:T(8,128)(2,1)} copy(bf16[256,8,2,512]{3,2,1,0:T(2,128)(2,1)} %bitcast.14) | data formatting | bytes 8388608
  23.9 0.1 pad_add_fusion.2.arrive
  24.0 23.3 %all-to-all-done.recv_ref = bf16[256,16,256]{2,1,0:T(8,128)(2,1)S(1)} async-done(((bf16[256,16,256]{2,1,0:T(8,128)(2,1)}), bf16[256,16,256]{2,1,0:T(8,128)(2,1)S(1)}, u32[]{:S(2)}, u32[]{:S(2)}) %all-to-all-start) | async-done | bytes 2097184 | tf_op jit(solution)/shard_map/all_to_all | solution.py:329
  47.3 0.1 broadcast_in_dim.35.cvec_ref
  47.5 1.2 %copy-done = bf16[2048,256]{1,0:T(8,128)(2,1)S(1)} copy-done((bf16[2048,256]{1,0:T(8,128)(2,1)S(1)}, bf16[2048,256]{1,0:T(8,128)(2,1)}, u32[]{:S(2)}) %copy-start) | copy-done | bytes 1048600
  48.7 23.7 %layer.1 = (bf16[128,72,128]{2,1,0:T(8,128)(2,1)}, f32[32,3,512]{2,1,0:T(4,128)S(1)}, f32[32,3,256]{2,1,0:T(4,128)S(1)}, f32[32,512,128]{2,1,0:T(8,128)}) custom-call(s32[64]{0:T(128)S(1)} %pad_add_fusion.2.arrive, bf16[256,16,256]{2,1,0:T(8,128)(2,1)S(1)} %all-to-all-done.recv_ref, bf16[2048,1024]{1,0:T(8,128)(2,1)} %bitcast.12, ...), custom_call_target="tpu_custom_call" | custom-call | tf_op jit(solution)/shard_map/layer/pallas_call | solution.py:343
  72.5 4.6 %all-to-all-start.1 = ((bf16[128,72,128]{2,1,0:T(8,128)(2,1)}), bf16[128,72,128]{2,1,0:T(8,128)(2,1)S(1)}, u32[]{:S(2)}, u32[]{:S(2)}) async-start(bf16[128,72,128]{2,1,0:T(8,128)(2,1)} %get-tuple-element.8), calls=%async_computation.1 | async-start | bytes 4718592 | tf_op jit(solution)/shard_map/all_to_all | solution.py:388
  77.1 0.7 copy.38
  77.7 0.7 copy.37
  78.5 31.7 %all-to-all-done.1.recv_ref = bf16[128,72,128]{2,1,0:T(8,128)(2,1)S(1)} async-done(((bf16[128,72,128]{2,1,0:T(8,128)(2,1)}), bf16[128,72,128]{2,1,0:T(8,128)(2,1)S(1)}, u32[]{:S(2)}, u32[]{:S(2)}) %all-to-all-start.1) | async-done | bytes 2359328 | tf_op jit(solution)/shard_map/all_to_all | solution.py:388
  110.2 1.4 %copy-done.6 = bf16[128,72,128]{2,1,0:T(8,128)(2,1)} copy-done((bf16[128,72,128]{2,1,0:T(8,128)(2,1)}, bf16[128,72,128]{2,1,0:T(8,128)(2,1)S(1)}, u32[]{:S(2)}) %copy-start.6) | copy-done | bytes 2359320
  111.6 5.6 %place_rows.1 = bf16[32,16,256]{2,1,0:T(8,128)(2,1)} custom-call(s32[64]{0:T(128)} %pad_add_fusion.1.info, bf16[128,72,128]{2,1,0:T(8,128)(2,1)} %copy-done.6), custom_call_target="tpu_custom_call" | custom-call | tf_op jit(solution)/shard_map/place_rows/pallas_call | solution.py:389
  (27 shorter events, 0.1 us)
Async XLA Ops:
  5.6 11.6 %copy-start.10 = (s32[512]{0:T(512)S(1)}, s32[512]{0:T(512)}, u32[]{:S(2)}) copy-start(s32[512]{0:T(512)} %param.31) | copy-start | bytes 6148
  5.6 11.6 %copy-start.11 = (s32[512]{0:T(512)S(1)}, s32[512]{0:T(512)}, u32[]{:S(2)}) copy-start(s32[512]{0:T(512)} %param.32) | copy-start | bytes 6148
  5.6 11.6 %copy-start.12 = (s32[512]{0:T(512)S(1)}, s32[512]{0:T(512)}, u32[]{:S(2)}) copy-start(s32[512]{0:T(512)} %param.33) | copy-start | bytes 6148
  5.6 11.7 %copy-start.13 = (f32[8]{0:T(128)S(1)}, f32[8]{0:T(128)}, u32[]{:S(2)}) copy-start(f32[8]{0:T(128)} %param.25) | copy-start | bytes 100
  5.6 12.4 %copy-start.8 = (f32[32,3,256]{2,0,1:T(8,128)S(1)}, f32[32,3,256]{2,0,1:T(8,128)}, u32[]{:S(2)}) copy-start(f32[32,3,256]{2,0,1:T(8,128)} %param.30) | copy-start | bytes 294916
  5.6 12.5 %copy-start.7 = (f32[32,3,512]{2,0,1:T(8,128)S(1)}, f32[32,3,512]{2,0,1:T(8,128)}, u32[]{:S(2)}) copy-start(f32[32,3,512]{2,0,1:T(8,128)} %param.29) | copy-start | bytes 589828
  5.6 12.6 %copy-start.9 = (bf16[2048,8]{0,1:T(8,128)(2,1)S(1)}, bf16[2048,8]{0,1:T(8,128)(2,1)}, u32[]{:S(2)}) copy-start(bf16[2048,8]{0,1:T(8,128)(2,1)} %param.20) | copy-start | bytes 98308
  5.6 41.7 %all-to-all-start = ((bf16[256,16,256]{2,1,0:T(8,128)(2,1)}), bf16[256,16,256]{2,1,0:T(8,128)(2,1)S(1)}, u32[]{:S(2)}, u32[]{:S(2)}) async-start(bf16[256,16,256]{2,1,0:T(8,128)(2,1)} %send_rows.1), calls=%async_computation | async-start | bytes 4194304 | tf_op jit(solution)/shard_map/all_to_all | solution.py:329
  18.5 28.9 %copy-start.1 = (f32[5,512]{1,0:T(8,128)S(1)}, f32[5,512]{1,0:T(8,128)}, u32[]{:S(2)}) copy-start(f32[5,512]{1,0:T(8,128)} %cxw_ref.1) | copy-start | bytes 30724
  18.5 28.9 %copy-start.2 = (f32[5,256]{1,0:T(8,128)S(1)}, f32[5,256]{1,0:T(8,128)}, u32[]{:S(2)}) copy-start(f32[5,256]{1,0:T(8,128)} %cbw_ref.1) | copy-start | bytes 15364
  18.5 28.9 %copy-start.3 = (f32[512]{0:T(512)S(1)}, f32[512]{0:T(512)}, u32[]{:S(2)}) copy-start(f32[512]{0:T(512)} %param.26) | copy-start | bytes 6148
  18.5 28.9 %copy-start.4 = (f32[8]{0:T(128)S(1)}, f32[8]{0:T(128)}, u32[]{:S(2)}) copy-start(f32[8]{0:T(128)} %param.23) | copy-start | bytes 100
  18.6 28.9 %copy-start.5 = (f32[8]{0:T(128)S(1)}, f32[8]{0:T(128)}, u32[]{:S(2)}) copy-start(f32[8]{0:T(128)} %param.24) | copy-start | bytes 100
  47.5 1.2 %copy-start = (bf16[2048,256]{1,0:T(8,128)(2,1)S(1)}, bf16[2048,256]{1,0:T(8,128)(2,1)}, u32[]{:S(2)}) copy-start(bf16[2048,256]{1,0:T(8,128)(2,1)} %wbc_ref.1) | copy-start | bytes 3145732
  72.5 37.7 %all-to-all-start.1 = ((bf16[128,72,128]{2,1,0:T(8,128)(2,1)}), bf16[128,72,128]{2,1,0:T(8,128)(2,1)S(1)}, u32[]{:S(2)}, u32[]{:S(2)}) async-start(bf16[128,72,128]{2,1,0:T(8,128)(2,1)} %get-tuple-element.8), calls=%async_computation.1 | async-start | bytes 4718592 | tf_op jit(solution)/shard_map/all_to_all | solution.py:388
  110.2 1.4 %copy-start.6 = (bf16[128,72,128]{2,1,0:T(8,128)(2,1)}, bf16[128,72,128]{2,1,0:T(8,128)(2,1)S(1)}, u32[]{:S(2)}) copy-start(bf16[128,72,128]{2,1,0:T(8,128)(2,1)S(1)} %all-to-all-done.1.recv_ref) | copy-start | bytes 7077892

commit v2 on v1

v2 whole, which is shorter than its diff:
```python
import functools

import jax
import jax.numpy as jnp
from jax import lax
from jax.experimental import pallas as pl
from jax.experimental.pallas import tpu as pltpu
from jax.sharding import PartitionSpec as P

f32 = jnp.float32
bf16 = jnp.bfloat16
NT = (((1,), (1,)), ((), ()))
TN = (((0,), (0,)), ((), ()))
STAT_ROWS = 8
MIB = 1024 * 1024
MIX_MIB = 36
STAGE_MIB = 14
STATE_MIB = 16


def send_kernel(slot_ref, hid_ref, out_hbm, buf, seen, order, sem, *, heads_dev):
    requests = hid_ref.shape[0]
    peers = seen.shape[0]
    first = lax.axis_index("req") * requests
    for o in range(peers):
        seen[o] = 0

    def find(i, carry):
        owner = lax.div(slot_ref[first + i], requests)
        j = seen[owner]
        seen[owner] = j + 1
        order[owner * 2 + j] = i
        return carry

    lax.fori_loop(0, requests, find, 0, unroll=4)

    def block(o):
        at = pl.ds(o * 2 * heads_dev, 2 * heads_dev)
        return pltpu.make_async_copy(buf.at[at], out_hbm.at[at], sem.at[o])

    def fill(o, carry):
        for j in range(2):
            rows = hid_ref[order[o * 2 + j]]
            for h in range(heads_dev):
                buf[(o * heads_dev + h) * 2 + j] = rows
        block(o).start()
        return carry

    lax.fori_loop(0, peers, fill, 0, unroll=2)
    lax.fori_loop(0, peers, lambda o, c: (block(o).wait(), c)[1], 0)


def stage_kernel(arrive, state_hbm, turned_hbm, st_ref, turned_ref, in_sem, out_sem):
    requests = turned_ref.shape[0]

    def load_state(i):
        return pltpu.make_async_copy(state_hbm.at[arrive[i]], st_ref.at[i], in_sem.at[i])

    def save(i):
        return pltpu.make_async_copy(turned_ref.at[i], turned_hbm.at[i], out_sem.at[i])

    lax.fori_loop(0, requests, lambda i, c: (load_state(i).start(), c)[1], 0)

    def body(i, carry):
        load_state(i).wait()
        turned_ref[i] = st_ref[i].astype(bf16).T
        save(i).start()
        return carry

    lax.fori_loop(0, requests, body, 0)
    lax.fori_loop(0, requests, lambda i, c: (save(i).wait(), c)[1], 0)


def split(x, terms):
    out = []
    for _ in range(terms - 1):
        out.append(x.astype(bf16))
        x = x - out[-1].astype(f32)
    return out + [x.astype(bf16)]


def mix_kernel(
    arrive,
    recv_ref,
    wdt_ref,
    cxw_ref,
    cbw_ref,
    bias_ref,
    alog_ref,
    skip_ref,
    gain_ref,
    cvec_ref,
    cx_ref,
    cb_ref,
    wzx_hbm,
    wbc_hbm,
    wout_hbm,
    turned_hbm,
    out_hbm,
    push_hbm,
    b_hbm,
    dec_hbm,
    xin_hbm,
    bin_hbm,
    xw_ref,
    bw_ref,
    gate_ref,
    ec_ref,
    sc_ref,
    fd_ref,
    g_ref,
    sq_ref,
    out_ref,
    push_ref,
    b_ref,
    xin_ref,
    bin_ref,
    wzx_ref,
    wbc_ref,
    wout_ref,
    turned_ref,
    dec_ref,
    out_sem,
    side_sem,
    weight_sem,
    *,
    heads_dev,
):
    requests = cx_ref.shape[0]
    tail = cx_ref.shape[1]
    inner = xw_ref.shape[2]
    steps = recv_ref.shape[1]
    part = recv_ref.shape[2]
    peers = recv_ref.shape[0] // (2 * heads_dev)
    tokens = requests * steps
    nstate = b_ref.shape[2]
    heads = wdt_ref.shape[1]
    headdim = inner // heads
    spread = heads * steps
    base = 8 - tail
    blk = 256
    blocks = inner // blk

    load_zx, load_bc, load_turned, load_out = [
        pltpu.make_async_copy(src, dst, weight_sem.at[n])
        for n, (src, dst) in enumerate(
            [(wzx_hbm, wzx_ref), (wbc_hbm, wbc_ref), (turned_hbm, turned_ref), (wout_hbm, wout_ref)]
        )
    ]
    for copy in (load_zx, load_bc, load_turned, load_out):
        copy.start()

    def previous(i, carry):
        row = arrive[i]
        xw_ref[i, base:8, :] = cx_ref[row]
        bw_ref[i, base:8, :] = cb_ref[row]
        return carry

    lax.fori_loop(0, requests, previous, 0, unroll=4)

    view = recv_ref.reshape(peers, heads_dev, 2, steps, part)
    tok = jnp.concatenate(
        [view[:, h].reshape(tokens, part) for h in range(heads_dev)], axis=1
    )

    def proj(w):
        return jnp.dot(tok, w, preferred_element_type=f32).astype(bf16)

    dt_in = proj(wdt_ref[...]).astype(f32)
    load_zx.wait()
    load_bc.wait()
    for n in range(blocks):
        cols = slice(n * blk, (n + 1) * blk)
        x_n = proj(wzx_ref[:, inner + n * blk : inner + (n + 1) * blk])
        xin_ref[:, :, cols] = x_n.reshape(requests, steps, blk)
        xw_ref[:, 8 : 8 + steps, cols] = x_n.astype(f32).reshape(requests, steps, blk)
    bc_n = proj(wbc_ref[...])
    bin_ref[...] = bc_n.reshape(requests, steps, 2 * nstate)
    bw_ref[:, 8 : 8 + steps, :] = bc_n.astype(f32).reshape(requests, steps, 2 * nstate)
    side = [
        pltpu.make_async_copy(xin_ref, xin_hbm, side_sem.at[0]),
        pltpu.make_async_copy(bin_ref, bin_hbm, side_sem.at[1]),
        pltpu.make_async_copy(push_ref, push_hbm, side_sem.at[2]),
        pltpu.make_async_copy(b_ref, b_hbm, side_sem.at[3]),
        pltpu.make_async_copy(dec_ref, dec_hbm, side_sem.at[4]),
    ]
    side[0].start()
    side[1].start()
    for n in range(blocks):
        gate_ref[:, n * blk : (n + 1) * blk] = proj(wzx_ref[:, n * blk : (n + 1) * blk])

    pre = dt_in + bias_ref[...]
    dt = jnp.maximum(pre, 0.0) + jnp.log1p(jnp.exp(-jnp.abs(pre)))
    rate = -dt * jnp.exp(alog_ref[...])
    place = lax.rem(lax.broadcasted_iota(jnp.int32, (tokens, heads), 0), steps)
    cumul = rate
    d = 1
    while d < steps:
        cumul = cumul + jnp.where(place >= d, pltpu.roll(cumul, d, 0), 0.0)
        d *= 2
    live = place < cvec_ref[...]
    total = jnp.sum(jnp.where(live, rate, 0.0).reshape(requests, steps, heads), axis=1, keepdims=True)
    dec_ref[...] = jnp.exp(total)
    totals = jnp.broadcast_to(total, (requests, steps, heads)).reshape(tokens, heads)
    scaled = jnp.where(live, jnp.exp(jnp.where(live, totals - cumul, 0.0)) * dt, 0.0)

    def widen(x, width, each, terms):
        rows = lax.broadcasted_iota(jnp.int32, (heads, width), 0)
        cols = lax.div(lax.broadcasted_iota(jnp.int32, (heads, width), 1), each)
        pick = (rows == cols).astype(bf16)
        wide = None
        for term in split(x, terms):
            more = jnp.dot(term, pick, preferred_element_type=f32)
            wide = more if wide is None else wide + more
        return wide.reshape(requests, steps, width)

    ec_ref[...] = widen(jnp.exp(cumul), inner, headdim, 2)
    sc_ref[...] = widen(scaled, inner, headdim, 2)
    cum2 = widen(cumul, spread, steps, 3)
    dt2 = widen(dt, spread, steps, 2)
    t_at = lax.broadcasted_iota(jnp.int32, (1, steps, spread), 1)
    s_at = lax.rem(lax.broadcasted_iota(jnp.int32, (1, steps, spread), 2), steps)
    same = t_at == s_at
    lower = t_at >= s_at
    crow = jnp.sum(jnp.where(same, cum2, 0.0), axis=1, keepdims=True)
    drow = jnp.sum(jnp.where(same, dt2, 0.0), axis=1, keepdims=True)
    fd_ref[...] = jnp.where(lower, jnp.exp(jnp.where(lower, cum2 - crow, 0.0)) * drow, 0.0)

    group = heads // 2
    gspread, ginner = group * steps, group * headdim
    r_head = lax.div(lax.broadcasted_iota(jnp.int32, (gspread, ginner), 0), steps)
    c_head = lax.div(lax.broadcasted_iota(jnp.int32, (gspread, ginner), 1), headdim)
    diag = (r_head == c_head).astype(bf16)
    many = 8
    rows = many * steps
    own = lax.div(lax.broadcasted_iota(jnp.int32, (rows, rows), 0), steps) == lax.div(
        lax.broadcasted_iota(jnp.int32, (rows, rows), 1), steps
    )
    repeat = (
        lax.rem(lax.broadcasted_iota(jnp.int32, (rows, spread), 0), steps)
        == lax.rem(lax.broadcasted_iota(jnp.int32, (rows, spread), 1), steps)
    ).astype(bf16)

    def conv(win_ref, w_ref, at):
        total_c = w_ref[tail + 1 : tail + 2, :][None]
        for k in range(tail + 1):
            total_c = total_c + w_ref[k : k + 1, :][None] * win_ref[at, base + k : base + k + steps, :]
        return (total_c * lax.logistic(total_c)).astype(bf16)

    def body(n, carry):
        at = pl.ds(n * many, many)
        x = conv(xw_ref, cxw_ref, at)
        bc = conv(bw_ref, cbw_ref, at)
        b_ref[at] = bc[:, :, :nstate]
        b = bc[:, :, :nstate].reshape(rows, nstate)
        c = bc[:, :, nstate:].reshape(rows, nstate)
        gram = jnp.where(own, lax.dot_general(c, b, NT, preferred_element_type=f32), 0.0)
        spread_gram = sum(jnp.dot(t, repeat, preferred_element_type=f32) for t in split(gram, 2))
        factor = (spread_gram * fd_ref[at].reshape(rows, spread)).astype(bf16)
        parts = []
        for r in range(many):
            tok_r = slice(r * steps, (r + 1) * steps)
            carried = jnp.dot(c[tok_r], turned_ref[n * many + r], preferred_element_type=f32)
            within = jnp.concatenate(
                [
                    jnp.dot(
                        factor[tok_r, g * gspread : (g + 1) * gspread],
                        jnp.concatenate([x[r, :, g * ginner : (g + 1) * ginner]] * group, axis=0)
                        * diag,
                        preferred_element_type=f32,
                    )
                    for g in range(2)
                ],
                axis=1,
            )
            parts.append(carried * ec_ref[n * many + r] + within)
        xf = x.astype(f32).reshape(rows, inner)
        mixed = (jnp.concatenate(parts, axis=0) + skip_ref[...] * xf).astype(bf16)
        push_ref[at] = (xf * sc_ref[at].reshape(rows, inner)).astype(bf16).reshape(many, steps, inner)
        tok_at = pl.ds(pl.multiple_of(n * rows, rows), rows)
        gate = gate_ref[tok_at, :].astype(f32)
        gated = mixed.astype(f32) * (gate * lax.logistic(gate))
        sq_ref[tok_at, :] = (gated * gated).astype(bf16)
        g_ref[tok_at, :] = (gated * gain_ref[...]).astype(bf16)
        return carry

    load_turned.wait()
    load_out.wait()
    lax.fori_loop(0, requests // many, body, 0)

    side[2].start()
    side[3].start()
    side[4].start()

    ones = jnp.ones((STAT_ROWS, inner), bf16)
    squares = lax.dot_general(ones, sq_ref[...], NT, preferred_element_type=f32)
    high = squares.astype(bf16).astype(f32)
    first = lax.broadcasted_iota(jnp.int32, squares.shape, 0) == 0
    stats = jnp.where(first, high, squares - high).astype(bf16)
    pair = 2 * steps
    data_rows = 2 * pair

    def leave(h):
        return pltpu.make_async_copy(out_ref.at[:, h], out_hbm.at[:, h], out_sem.at[h])

    for b in range(peers):
        piece = jnp.concatenate(
            [stats[:, b * pair : (b + 1) * pair], jnp.zeros((STAT_ROWS, 128 - pair), bf16)], axis=1
        )
        for h in range(heads_dev):
            out_ref[b, h, data_rows:, :] = piece

    for h in range(heads_dev):
        res = jnp.dot(
            g_ref[...], wout_ref[:, h * part : (h + 1) * part], preferred_element_type=f32
        ).astype(bf16)
        out_ref[:, h, 0:pair, :] = res[:, :128].reshape(peers, pair, 128)
        out_ref[:, h, pair:data_rows, :] = res[:, 128:].reshape(peers, pair, 128)
        leave(h).start()
    for h in range(heads_dev):
        leave(h).wait()
    for copy in side:
        copy.wait()


def state_kernel(
    arrive,
    push_ref,
    b_ref,
    dec_ref,
    xin_ref,
    bin_ref,
    cx_ref,
    cb_ref,
    state_hbm,
    newstate_hbm,
    ncx_ref,
    ncb_ref,
    xw_ref,
    bw_ref,
    st_ref,
    in_sem,
    out_sem,
):
    requests, steps, inner = push_ref.shape
    tail = ncx_ref.shape[1]
    nstate = b_ref.shape[2]
    heads = dec_ref.shape[2]
    headdim = inner // heads
    base = 8 - tail

    def load_state(i):
        return pltpu.make_async_copy(state_hbm.at[arrive[i]], st_ref.at[i], in_sem.at[i])

    def save_state(i):
        return pltpu.make_async_copy(st_ref.at[i], newstate_hbm.at[arrive[i]], out_sem.at[i])

    lax.fori_loop(0, requests, lambda i, c: (load_state(i).start(), c)[1], 0)

    def body(i, carry):
        row = arrive[i]
        back = steps + tail - arrive[requests + i]
        xw_ref[i, base:8, :] = cx_ref[row]
        xw_ref[i, 8:, :] = xin_ref[i].astype(f32)
        bw_ref[i, base:8, :] = cb_ref[row]
        bw_ref[i, 8:, :] = bin_ref[i].astype(f32)
        ncx_ref[row] = pltpu.roll(xw_ref[i], back, 0)[:tail]
        ncb_ref[row] = pltpu.roll(bw_ref[i], back, 0)[:tail]
        update = lax.dot_general(push_ref[i], b_ref[i], TN, preferred_element_type=f32)
        dec = dec_ref[i]
        load_state(i).wait()
        for h in range(heads):
            sl = slice(h * headdim, (h + 1) * headdim)
            factor_h = jnp.broadcast_to(dec[:, h : h + 1], (headdim, nstate))
            st_ref[i, sl, :] = factor_h * st_ref[i, sl, :] + update[sl, :]
        save_state(i).start()
        return carry

    lax.fori_loop(0, requests, body, 0)
    lax.fori_loop(0, requests, lambda i, c: (save_state(i).wait(), c)[1], 0)


def final_kernel(slot_ref, len_ref, recv_ref, out_ref, seen, *, heads_dev, inner_all):
    requests, steps, part = out_ref.shape
    peers = seen.shape[0]
    pair = 2 * steps
    data_rows = 2 * pair
    base = lax.axis_index("req") * requests
    for o in range(peers):
        seen[o] = 0
    view = recv_ref.reshape(peers, heads_dev, data_rows + STAT_ROWS, 128)
    place = lax.broadcasted_iota(jnp.int32, (steps, 128), 0)
    lane = lax.broadcasted_iota(jnp.int32, (steps, 128), 1)

    def body(i, carry):
        owner = lax.div(slot_ref[base + i], requests)
        length = len_ref[base + i]
        j = seen[owner]
        seen[owner] = j + 1
        stats = view[owner, 0, data_rows:, :].astype(f32)
        for h in range(1, heads_dev):
            stats = stats + view[owner, h, data_rows:, :].astype(f32)
        squares = stats[0:1, :] + stats[1:2, :]
        total = jnp.sum(jnp.where(lane == place + j * steps, squares, 0.0), axis=1, keepdims=True)
        scale = jnp.where(place < length, lax.rsqrt(total / inner_all + 1e-05), 0.0)
        for half in range(2):
            rows = pl.ds(pl.multiple_of(half * pair + j * steps, steps), steps)
            acc = view[owner, 0, rows, :].astype(f32)
            for h in range(1, heads_dev):
                acc = acc + view[owner, h, rows, :].astype(f32)
            out_ref[i, :, half * 128 : (half + 1) * 128] = jnp.where(
                place < length, acc * scale, 0.0
            ).astype(bf16)
        return carry

    lax.fori_loop(0, requests, body, 0, unroll=4)


def vmem(n):
    return [pl.BlockSpec(memory_space=pltpu.VMEM)] * n


def smem():
    return pl.BlockSpec(memory_space=pltpu.SMEM)


def hbm(n):
    return [pl.BlockSpec(memory_space=pltpu.HBM)] * n


def in_hbm(x):
    return pltpu.with_memory_space_constraint(x, pltpu.HBM)


def per_device(
    hidden,
    w_zx,
    w_bc,
    w_dt,
    conv_x_w,
    conv_bc_w,
    dt_bias,
    a_log,
    d_skip,
    norm_gain,
    w_out,
    ssm_state,
    conv_x_state,
    conv_bc_state,
    slot,
    lengths,
    accepted,
):
    requests, steps, part = hidden.shape
    width = w_zx.shape[0]
    inner = w_zx.shape[2]
    bc_cols = w_bc.shape[1]
    heads = w_dt.shape[1]
    headdim = inner // heads
    nstate = bc_cols // 2
    tail = conv_x_state.shape[1]
    peers = lax.axis_size("req")
    heads_dev = lax.axis_size("head")
    tokens = requests * steps
    spread = heads * steps
    out_rows = 4 * steps + STAT_ROWS
    me = lax.axis_index("req")

    slot_blocks = slot.reshape(peers, requests)
    outgoing = pl.pallas_call(
        functools.partial(send_kernel, heads_dev=heads_dev),
        out_shape=pltpu.HBM((peers * heads_dev * 2, steps, part), bf16),
        in_specs=[smem()] + vmem(1),
        out_specs=hbm(1)[0],
        scratch_shapes=[
            pltpu.VMEM((peers * heads_dev * 2, steps, part), bf16),
            pltpu.SMEM((peers,), jnp.int32),
            pltpu.SMEM((requests,), jnp.int32),
            pltpu.SemaphoreType.DMA((peers,)),
        ],
        compiler_params=pltpu.CompilerParams(vmem_limit_bytes=4 * MIB),
        name="send_rows",
    )(in_hbm(slot), in_hbm(hidden))
    arrived = lax.all_to_all(outgoing, ("req", "head"), split_axis=0, concat_axis=0, tiled=True)

    counted = jnp.minimum(accepted, lengths).reshape(peers, requests)
    order = jnp.arange(requests, dtype=jnp.int32)[None, :]
    code = (order * requests + slot_blocks % requests) * (2 * steps) + counted
    here = slot_blocks // requests == me
    low = jnp.min(jnp.where(here, code, jnp.iinfo(jnp.int32).max), axis=1)
    high = jnp.max(jnp.where(here, code, -1), axis=1)
    both = jnp.stack([low, high], axis=1).reshape(requests)
    rows = (both // (2 * steps)) % requests
    counts = both % (2 * steps)
    arrive = jnp.concatenate([rows, counts])
    count_col = jnp.broadcast_to(counts[:, None, None], (requests, steps, heads)).reshape(tokens, heads)

    states = in_hbm(ssm_state.reshape(requests, inner, nstate))
    turned = pl.pallas_call(
        stage_kernel,
        out_shape=pltpu.HBM((requests, nstate, inner), bf16),
        in_specs=[smem()] + hbm(1),
        out_specs=hbm(1)[0],
        scratch_shapes=[
            pltpu.VMEM((requests, inner, nstate), f32),
            pltpu.VMEM((requests, nstate, inner), bf16),
            pltpu.SemaphoreType.DMA((requests,)),
            pltpu.SemaphoreType.DMA((requests,)),
        ],
        compiler_params=pltpu.CompilerParams(vmem_limit_bytes=STAGE_MIB * MIB),
        cost_estimate=pl.CostEstimate(flops=10**9, bytes_accessed=20 * MIB, transcendentals=0),
        name="stage",
    )(arrive, states)
    leaving, push, b_conv, decay, x_in, bc_in = pl.pallas_call(
        functools.partial(mix_kernel, heads_dev=heads_dev),
        out_shape=(
            pltpu.HBM((peers, heads_dev, out_rows, 128), bf16),
            pltpu.HBM((requests, steps, inner), bf16),
            pltpu.HBM((requests, steps, nstate), bf16),
            pltpu.HBM((requests, 1, heads), f32),
            pltpu.HBM((requests, steps, inner), bf16),
            pltpu.HBM((requests, steps, bc_cols), bf16),
        ),
        in_specs=[smem()] + vmem(11) + hbm(4),
        out_specs=tuple(hbm(6)),
        scratch_shapes=[
            pltpu.VMEM((requests, 8 + steps, inner), f32),
            pltpu.VMEM((requests, 8 + steps, bc_cols), f32),
            pltpu.VMEM((tokens, inner), bf16),
            pltpu.VMEM((requests, steps, inner), f32),
            pltpu.VMEM((requests, steps, inner), f32),
            pltpu.VMEM((requests, steps, spread), f32),
            pltpu.VMEM((tokens, inner), bf16),
            pltpu.VMEM((tokens, inner), bf16),
            pltpu.VMEM((peers, heads_dev, out_rows, 128), bf16),
            pltpu.VMEM((requests, steps, inner), bf16),
            pltpu.VMEM((requests, steps, nstate), bf16),
            pltpu.VMEM((requests, steps, inner), bf16),
            pltpu.VMEM((requests, steps, bc_cols), bf16),
            pltpu.VMEM((width, 2 * inner), bf16),
            pltpu.VMEM((width, bc_cols), bf16),
            pltpu.VMEM((inner, width), bf16),
            pltpu.VMEM((requests, nstate, inner), bf16),
            pltpu.VMEM((requests, 1, heads), f32),
            pltpu.SemaphoreType.DMA((heads_dev,)),
            pltpu.SemaphoreType.DMA((5,)),
            pltpu.SemaphoreType.DMA((4,)),
        ],
        compiler_params=pltpu.CompilerParams(vmem_limit_bytes=MIX_MIB * MIB),
        cost_estimate=pl.CostEstimate(flops=4 * 10**9, bytes_accessed=8 * MIB, transcendentals=10**6),
        name="mix",
    )(
        arrive,
        arrived,
        w_dt,
        conv_x_w,
        conv_bc_w,
        dt_bias[None, :],
        a_log[None, :],
        jnp.repeat(d_skip, headdim)[None, :],
        norm_gain[None, :],
        count_col,
        conv_x_state,
        conv_bc_state,
        in_hbm(w_zx.reshape(width, 2 * inner)),
        in_hbm(w_bc),
        in_hbm(w_out),
        in_hbm(turned),
    )
    leaving = leaving.reshape(peers * heads_dev, out_rows, 128)
    returned = lax.all_to_all(leaving, ("req", "head"), split_axis=0, concat_axis=0, tiled=True)
    new_state, new_conv_x, new_conv_bc = pl.pallas_call(
        state_kernel,
        out_shape=(
            pltpu.HBM((requests, inner, nstate), f32),
            jax.ShapeDtypeStruct(conv_x_state.shape, f32),
            jax.ShapeDtypeStruct(conv_bc_state.shape, f32),
        ),
        in_specs=[smem()] + vmem(7) + hbm(1),
        out_specs=tuple(hbm(1) + vmem(2)),
        scratch_shapes=[
            pltpu.VMEM((requests, 8 + steps, inner), f32),
            pltpu.VMEM((requests, 8 + steps, bc_cols), f32),
            pltpu.VMEM((requests, inner, nstate), f32),
            pltpu.SemaphoreType.DMA((requests,)),
            pltpu.SemaphoreType.DMA((requests,)),
        ],
        compiler_params=pltpu.CompilerParams(vmem_limit_bytes=STATE_MIB * MIB),
        cost_estimate=pl.CostEstimate(flops=2 * 10**9, bytes_accessed=20 * MIB, transcendentals=0),
        name="update",
    )(arrive, push, b_conv, decay, x_in, bc_in, conv_x_state, conv_bc_state, states)
    out = pl.pallas_call(
        functools.partial(final_kernel, heads_dev=heads_dev, inner_all=inner * heads_dev),
        out_shape=jax.ShapeDtypeStruct((requests, steps, part), bf16),
        in_specs=[smem(), smem()] + vmem(1),
        out_specs=vmem(1)[0],
        scratch_shapes=[pltpu.SMEM((peers,), jnp.int32)],
        compiler_params=pltpu.CompilerParams(vmem_limit_bytes=4 * MIB),
        name="place_rows",
    )(slot, lengths, returned)
    return (out, new_state.reshape(ssm_state.shape), new_conv_x, new_conv_bc)


def solution(mesh):
    in_specs = (
        P("req", None, "head"),
        P(None, None, "head"),
        P(),
        P(None, "head"),
        P(None, "head"),
        P(),
        P("head"),
        P("head"),
        P("head"),
        P("head"),
        P("head", None),
        P("req", "head", None, None),
        P("req", None, "head"),
        P("req", None, None),
        P(),
        P(),
        P(),
    )
    out_specs = (
        P("req", None, "head"),
        P("req", "head", None, None),
        P("req", None, "head"),
        P("req", None, None),
    )
    return jax.shard_map(
        per_device, mesh=mesh, in_specs=in_specs, out_specs=out_specs, check_vma=False
    )
```

time: 118 us -> 98.9 us (0.84)
  waiting for transfers between devices: 55 us -> 33.3 us
  Pallas kernels: 32.1 us -> 37.1 us
  local copies, waits for them, and re-layouts: 12.2 us -> 10.7 us
    all_to_all x1, waiting for transfers between devices: 31.7 us -> 16.2 us  [per_device(): lax.all_to_all(leaving, ('req', 'head'), split_axis=0, concat_axis=0, til...]
    pallas_call x1 -> x3, Pallas kernels: 23.7 us -> 32 us  [the longest x1 13 us: per_device(): pl.pallas_call(functools.partial(mix_kernel, heads_dev=heads_dev), out_sh...]
    all_to_all x1, waiting for transfers between devices: 23.3 us -> 17.1 us  [per_device(): lax.all_to_all(outgoing, ('req', 'head'), split_axis=0, concat_axis=0, ti...]
    pallas_call x1, Pallas kernels: 5.63 us -> 2.28 us  [per_device(): pl.pallas_call(functools.partial(final_kernel, heads_dev=heads_dev, inner...]
    dynamic_slice x2 -> x0, local copies, waits for them, and re-layouts: 1.51 us -> none  [the longest x1 0.76 us: per_device(): lax.dynamic_slice_in_dim(slot, me * requests, requests)]
    unnamed x34 -> x40, local copies, waits for them, and re-layouts: 9.96 us -> 9.99 us
  transfers between devices with their start and end apart: 2 -> 2, of which waited for: 2 -> 2; matrix products, arithmetic and copies ran while one was open for 7% -> 8% of each run, Pallas kernels for 0% -> 19%
where the time goes in v2:
time: 98.9 us; the launch traced here: 98.5 us
  Pallas kernels  37.1 us (38%)
  waiting for transfers between devices  33.3 us (34%)
  starting transfers between devices  16.2 us (16%)
  local copies, waits for them, and re-layouts  10.7 us (11%)
    all_to_all x1, waiting for transfers between devices, per_device(): lax.all_to_all(outgoing, ('req', 'head'), split_axis=0, concat_axis=0, ti...  17.1 us
    all_to_all x1, waiting for transfers between devices, per_device(): lax.all_to_all(leaving, ('req', 'head'), split_axis=0, concat_axis=0, til...  16.2 us
    pallas_call x1, Pallas kernels, per_device(): pl.pallas_call(functools.partial(mix_kernel, heads_dev=heads_dev), out_sh...  13 us
    pallas_call x1, Pallas kernels, per_device(): pl.pallas_call(state_kernel, out_shape=(pltpu.HBM((requests, inner, nstat...  12.8 us
    all_to_all x1, starting transfers between devices, per_device(): lax.all_to_all(outgoing, ('req', 'head'), split_axis=0, concat_axis=0, ti...  11.5 us
    unnamed x40, local copies, waits for them, and re-layouts  9.99 us
    pallas_call x1, Pallas kernels, per_device(): pl.pallas_call(stage_kernel, out_shape=pltpu.HBM((requests, nstate, inner...  6.26 us
    all_to_all x1, starting transfers between devices, per_device(): lax.all_to_all(leaving, ('req', 'head'), split_axis=0, concat_axis=0, til...  4.74 us
  transfers between devices with their start and end apart: 2, of which 2 were waited for; matrix products, arithmetic and copies ran while one was open for 8% of the time, Pallas kernels for 19%

profile of v2, /device:TPU:1, one launch (start us, length us, event | category | flops | bytes accessed | tf_op | source)
XLA Modules:
  0.0 98.5 jit_solution(9358363773193397748)
XLA Ops:
  0.7 2.8 %send_rows.1 = bf16[256,16,256]{2,1,0:T(8,128)(2,1)} custom-call(s32[512]{0:T(512)} %slot_ref.3, bf16[32,16,256]{2,1,0:T(8,128)(2,1)} %hid_ref.1), custom_call_target="tpu_custom_call" | custom-call | tf_op jit(solution)/shard_map/send_rows/pallas_call | solution.py:470
  3.5 11.5 %all-to-all-start = ((bf16[256,16,256]{2,1,0:T(8,128)(2,1)}), bf16[256,16,256]{2,1,0:T(8,128)(2,1)S(1)}, u32[]{:S(2)}, u32[]{:S(2)}) async-start(bf16[256,16,256]{2,1,0:T(8,128)(2,1)} %send_rows.1), calls=%async_computation | async-start | bytes 4194304 | tf_op jit(solution)/shard_map/all_to_all | solution.py:484
  15.0 0.1 reshape.57
  15.1 0.1 broadcast_in_dim.31
  15.1 0.1 broadcast_in_dim_reshape.3.skip_ref
  15.2 0.1 reshape.58
  15.3 0.1 select_reduce_fusion.1
  15.5 0.1 copy.37
  15.5 0.1 reshape.59
  15.7 0.1 broadcast_in_dim.33
  15.7 0.1 broadcast_in_dim.34
  15.8 0.1 copy.40.cb_ref
  15.9 0.0 copy-done.12
  15.9 0.1 copy.39.cx_ref
  16.1 0.3 copy.38.wdt_ref
  16.3 5.4 %copy.45 = bf16[256,8,2,512]{3,1,2,0:T(8,128)(2,1)} copy(bf16[256,8,2,512]{3,2,1,0:T(2,128)(2,1)} %bitcast.16) | data formatting | bytes 8388608
  21.7 0.1 pad_add_fusion.1.arrive
  21.8 0.0 copy-start.11
  21.8 6.3 %stage.1.turned_hbm = bf16[32,128,512]{2,1,0:T(8,128)(2,1)} custom-call(s32[64]{0:T(128)S(1)} %pad_add_fusion.1.arrive, f32[32,512,128]{2,1,0:T(8,128)} %bitcast.13), custom_call_target="tpu_custom_call" | custom-call | flops 1000000000 | bytes 20971520 | tf_op jit(solution)/shard_map/stage/pallas_call | solution.py:499
  28.1 17.1 %all-to-all-done.recv_ref = bf16[256,16,256]{2,1,0:T(8,128)(2,1)S(1)} async-done(((bf16[256,16,256]{2,1,0:T(8,128)(2,1)}), bf16[256,16,256]{2,1,0:T(8,128)(2,1)S(1)}, u32[]{:S(2)}, u32[]{:S(2)}) %all-to-all-start) | async-done | bytes 2097184 | tf_op jit(solution)/shard_map/all_to_all | solution.py:484
  45.2 0.1 broadcast_in_dim.35.cvec_ref
  45.3 13.0 %mix.1 = (bf16[16,8,72,128]{3,2,1,0:T(8,128)(2,1)}, bf16[32,16,512]{2,1,0:T(8,128)(2,1)}, bf16[32,16,128]{2,1,0:T(8,128)(2,1)}, f32[32,1,8]{2,1,0:T(1,128)}, bf1...) custom-call(s32[64]{0:T(128)S(1)} %pad_add_fusion.1.arrive, bf16[256,16,256]{2,1,0:T(8,128)(2,1)S(1)} %all-to-all-done.recv_ref, ...), custom_call_target="tpu_custom_call" | custom-call | flops 4000000000 | bytes 8388608 | tf_op jit(solution)/shard_map/mix/pallas_call | solution.py:514
  58.3 0.0 copy-start.2
  58.3 4.7 %all-to-all-start.1 = ((bf16[128,72,128]{2,1,0:T(8,128)(2,1)}), bf16[128,72,128]{2,1,0:T(8,128)(2,1)S(1)}, u32[]{:S(2)}, u32[]{:S(2)}) async-start(bf16[128,72,128]{2,1,0:T(8,128)(2,1)} %bitcast.17), calls=%async_computation.1 | async-start | bytes 4718592 | tf_op jit(solution)/shard_map/all_to_all | solution.py:571
  63.1 1.0 %copy-done.1 = bf16[32,16,512]{2,1,0:T(8,128)(2,1)S(1)} copy-done((bf16[32,16,512]{2,1,0:T(8,128)(2,1)S(1)}, bf16[32,16,512]{2,1,0:T(8,128)(2,1)}, u32[]{:S(2)}) %copy-start.1) | copy-done | bytes 524312
  64.2 0.9 copy-done.3
  65.1 0.7 copy-done.5
  65.8 12.8 %update.1 = (f32[32,512,128]{2,1,0:T(8,128)}, f32[32,3,512]{2,1,0:T(4,128)S(1)}, f32[32,3,256]{2,1,0:T(4,128)S(1)}) custom-call(s32[64]{0:T(128)S(1)} %pad_add_fusion.1.arrive, bf16[32,16,512]{2,1,0:T(8,128)(2,1)S(1)} %copy-done, bf16[32,16,128]{2,1,0:T(8,128)(2,1)S(1)} %copy-done.3, f32[32,1,8]{2,1,0:T(1,128)S(1)} %copy-done.5, ...), custom_call_target="tpu_custom_call" | custom-call | flops 2000000000 | bytes 20971520 | tf_op jit(solution)/shard_map/update/pallas_call | solution.py:572
  78.6 0.7 copy.44
  79.2 0.7 copy.43
  80.0 16.2 %all-to-all-done.1.recv_ref = bf16[128,72,128]{2,1,0:T(8,128)(2,1)S(1)} async-done(((bf16[128,72,128]{2,1,0:T(8,128)(2,1)}), bf16[128,72,128]{2,1,0:T(8,128)(2,1)S(1)}, u32[]{:S(2)}, u32[]{:S(2)}) %all-to-all-start.1) | async-done | bytes 2359328 | tf_op jit(solution)/shard_map/all_to_all | solution.py:571
  96.2 2.3 %place_rows.1 = bf16[32,16,256]{2,1,0:T(8,128)(2,1)} custom-call(s32[512]{0:T(512)S(1)} %copy-done.4, s32[512]{0:T(512)S(1)} %copy-done.8, bf16[128,72,128]{2,1,0:T(8,128)(2,1)S(1)} %all-to-all-done.1.recv_ref), custom_call_target="tpu_custom_call" | custom-call | tf_op jit(solution)/shard_map/place_rows/pallas_call | solution.py:592
  (32 shorter events, 0.1 us)
Async XLA Ops:
  0.6 14.4 %copy-start.4 = (s32[512]{0:T(512)S(1)}, s32[512]{0:T(512)}, u32[]{:S(2)}) copy-start(s32[512]{0:T(512)} %slot_ref.3) | copy-start | bytes 6148
  0.6 14.4 %copy-start.16 = (f32[8]{0:T(128)S(1)}, f32[8]{0:T(128)}, u32[]{:S(2)}) copy-start(f32[8]{0:T(128)} %param.25) | copy-start | bytes 100
  0.7 14.6 %copy-start.8 = (s32[512]{0:T(512)S(1)}, s32[512]{0:T(512)}, u32[]{:S(2)}) copy-start(s32[512]{0:T(512)} %len_ref.1) | copy-start | bytes 6148
  0.7 14.6 %copy-start.15 = (s32[512]{0:T(512)S(1)}, s32[512]{0:T(512)}, u32[]{:S(2)}) copy-start(s32[512]{0:T(512)} %param.33) | copy-start | bytes 6148
  0.7 15.1 %copy-start.13 = (f32[32,3,256]{2,0,1:T(8,128)S(1)}, f32[32,3,256]{2,0,1:T(8,128)}, u32[]{:S(2)}) copy-start(f32[32,3,256]{2,0,1:T(8,128)} %param.30) | copy-start | bytes 294916
  0.7 15.2 %copy-start.12 = (f32[32,3,512]{2,0,1:T(8,128)S(1)}, f32[32,3,512]{2,0,1:T(8,128)}, u32[]{:S(2)}) copy-start(f32[32,3,512]{2,0,1:T(8,128)} %param.29) | copy-start | bytes 589828
  0.7 15.4 %copy-start.14 = (bf16[2048,8]{0,1:T(8,128)(2,1)S(1)}, bf16[2048,8]{0,1:T(8,128)(2,1)}, u32[]{:S(2)}) copy-start(bf16[2048,8]{0,1:T(8,128)(2,1)} %param.20) | copy-start | bytes 98308
  3.5 41.7 %all-to-all-start = ((bf16[256,16,256]{2,1,0:T(8,128)(2,1)}), bf16[256,16,256]{2,1,0:T(8,128)(2,1)S(1)}, u32[]{:S(2)}, u32[]{:S(2)}) async-start(bf16[256,16,256]{2,1,0:T(8,128)(2,1)} %send_rows.1), calls=%async_computation | async-start | bytes 4194304 | tf_op jit(solution)/shard_map/all_to_all | solution.py:484
  21.8 23.5 %copy-start.6 = (f32[5,512]{1,0:T(8,128)S(1)}, f32[5,512]{1,0:T(8,128)}, u32[]{:S(2)}) copy-start(f32[5,512]{1,0:T(8,128)} %cxw_ref.1) | copy-start | bytes 30724
  21.8 23.5 %copy-start.7 = (f32[5,256]{1,0:T(8,128)S(1)}, f32[5,256]{1,0:T(8,128)}, u32[]{:S(2)}) copy-start(f32[5,256]{1,0:T(8,128)} %cbw_ref.1) | copy-start | bytes 15364
  21.8 23.5 %copy-start.9 = (f32[512]{0:T(512)S(1)}, f32[512]{0:T(512)}, u32[]{:S(2)}) copy-start(f32[512]{0:T(512)} %param.26) | copy-start | bytes 6148
  21.8 23.5 %copy-start.10 = (f32[8]{0:T(128)S(1)}, f32[8]{0:T(128)}, u32[]{:S(2)}) copy-start(f32[8]{0:T(128)} %param.23) | copy-start | bytes 100
  21.8 23.5 %copy-start.11 = (f32[8]{0:T(128)S(1)}, f32[8]{0:T(128)}, u32[]{:S(2)}) copy-start(f32[8]{0:T(128)} %param.24) | copy-start | bytes 100
  58.3 4.8 %copy-start = (bf16[32,16,512]{2,1,0:T(8,128)(2,1)S(1)}, bf16[32,16,512]{2,1,0:T(8,128)(2,1)}, u32[]{:S(2)}) copy-start(bf16[32,16,512]{2,1,0:T(8,128)(2,1)} %get-tuple-element.14.push_ref) | copy-start | bytes 1572868
  58.3 4.8 %copy-start.2 = (bf16[32,16,256]{2,1,0:T(8,128)(2,1)S(1)}, bf16[32,16,256]{2,1,0:T(8,128)(2,1)}, u32[]{:S(2)}) copy-start(bf16[32,16,256]{2,1,0:T(8,128)(2,1)} %get-tuple-element.18.bin_ref) | copy-start | bytes 786436
  58.3 37.8 %all-to-all-start.1 = ((bf16[128,72,128]{2,1,0:T(8,128)(2,1)}), bf16[128,72,128]{2,1,0:T(8,128)(2,1)S(1)}, u32[]{:S(2)}, u32[]{:S(2)}) async-start(bf16[128,72,128]{2,1,0:T(8,128)(2,1)} %bitcast.17), calls=%async_computation.1 | async-start | bytes 4718592 | tf_op jit(solution)/shard_map/all_to_all | solution.py:571
  63.1 1.0 %copy-start.1 = (bf16[32,16,512]{2,1,0:T(8,128)(2,1)S(1)}, bf16[32,16,512]{2,1,0:T(8,128)(2,1)}, u32[]{:S(2)}) copy-start(bf16[32,16,512]{2,1,0:T(8,128)(2,1)} %get-tuple-element.17.xin_ref) | copy-start | bytes 1572868
  64.2 0.9 copy-start.3
  65.1 0.7 copy-start.5

commit v3 on v2

--- a/solution.py
+++ b/solution.py
@@ -11,42 +11,41 @@
 bf16 = jnp.bfloat16
 NT = (((1,), (1,)), ((), ()))
 TN = (((0,), (0,)), ((), ()))
-STAT_ROWS = 8
+STAT_ROWS = 4
 MIB = 1024 * 1024
 MIX_MIB = 36
 STAGE_MIB = 14
 STATE_MIB = 16
 
 
-def send_kernel(slot_ref, hid_ref, out_hbm, buf, seen, order, sem, *, heads_dev):
+def visit(slot_ref, first, requests, act):
+    def body(i, met):
+        owner = lax.div(slot_ref[first + i], requests)
+        bit = lax.shift_left(jnp.int32(1), owner)
+        act(i, owner, lax.min(met & bit, 1))
+        return met | bit
+
+    lax.fori_loop(0, requests, body, jnp.int32(0), unroll=8)
+
+
+def send_kernel(slot_ref, hid_ref, out_hbm, buf, sem, *, heads_dev):
     requests = hid_ref.shape[0]
-    peers = seen.shape[0]
-    first = lax.axis_index("req") * requests
-    for o in range(peers):
-        seen[o] = 0
-
-    def find(i, carry):
-        owner = lax.div(slot_ref[first + i], requests)
-        j = seen[owner]
-        seen[owner] = j + 1
-        order[owner * 2 + j] = i
-        return carry
-
-    lax.fori_loop(0, requests, find, 0, unroll=4)
+    peers = buf.shape[0] // (2 * heads_dev)
 
     def block(o):
         at = pl.ds(o * 2 * heads_dev, 2 * heads_dev)
         return pltpu.make_async_copy(buf.at[at], out_hbm.at[at], sem.at[o])
 
-    def fill(o, carry):
-        for j in range(2):
-            rows = hid_ref[order[o * 2 + j]]
-            for h in range(heads_dev):
-                buf[(o * heads_dev + h) * 2 + j] = rows
-        block(o).start()
-        return carry
-
-    lax.fori_loop(0, peers, fill, 0, unroll=2)
+    def place(i, owner, j):
+        rows = hid_ref[i]
+        for h in range(heads_dev):
+            buf[(owner * heads_dev + h) * 2 + j] = rows
+
+        @pl.when(j == 1)
+        def _():
+            block(owner).start()
+
+    visit(slot_ref, lax.axis_index("req") * requests, requests, place)
     lax.fori_loop(0, peers, lambda o, c: (block(o).wait(), c)[1], 0)
 
 
@@ -141,13 +140,20 @@
     blk = 256
     blocks = inner // blk
 
-    load_zx, load_bc, load_turned, load_out = [
+    z_cols, x_cols = pl.ds(0, inner), pl.ds(inner, inner)
+    load_x, load_bc, load_z, load_turned, load_out = [
         pltpu.make_async_copy(src, dst, weight_sem.at[n])
         for n, (src, dst) in enumerate(
-            [(wzx_hbm, wzx_ref), (wbc_hbm, wbc_ref), (turned_hbm, turned_ref), (wout_hbm, wout_ref)]
+            [
+                (wzx_hbm.at[:, x_cols], wzx_ref.at[:, x_cols]),
+                (wbc_hbm, wbc_ref),
+                (wzx_hbm.at[:, z_cols], wzx_ref.at[:, z_cols]),
+                (turned_hbm, turned_ref),
+                (wout_hbm, wout_ref),
+            ]
         )
     ]
-    for copy in (load_zx, load_bc, load_turned, load_out):
+    for copy in (load_x, load_bc, load_z, load_turned, load_out):
         copy.start()
 
     def previous(i, carry):
@@ -167,7 +173,7 @@
         return jnp.dot(tok, w, preferred_element_type=f32).astype(bf16)
 
     dt_in = proj(wdt_ref[...]).astype(f32)
-    load_zx.wait()
+    load_x.wait()
     load_bc.wait()
     for n in range(blocks):
         cols = slice(n * blk, (n + 1) * blk)
@@ -186,6 +192,7 @@
     ]
     side[0].start()
     side[1].start()
+    load_z.wait()
     for n in range(blocks):
         gate_ref[:, n * blk : (n + 1) * blk] = proj(wzx_ref[:, n * blk : (n + 1) * blk])
 
@@ -247,8 +254,8 @@
             total_c = total_c + w_ref[k : k + 1, :][None] * win_ref[at, base + k : base + k + steps, :]
         return (total_c * lax.logistic(total_c)).astype(bf16)
 
-    def body(n, carry):
-        at = pl.ds(n * many, many)
+    def body(n):
+        at = slice(n * many, (n + 1) * many)
         x = conv(xw_ref, cxw_ref, at)
         bc = conv(bw_ref, cbw_ref, at)
         b_ref[at] = bc[:, :, :nstate]
@@ -277,22 +284,22 @@
         xf = x.astype(f32).reshape(rows, inner)
         mixed = (jnp.concatenate(parts, axis=0) + skip_ref[...] * xf).astype(bf16)
         push_ref[at] = (xf * sc_ref[at].reshape(rows, inner)).astype(bf16).reshape(many, steps, inner)
-        tok_at = pl.ds(pl.multiple_of(n * rows, rows), rows)
+        tok_at = slice(n * rows, (n + 1) * rows)
         gate = gate_ref[tok_at, :].astype(f32)
         gated = mixed.astype(f32) * (gate * lax.logistic(gate))
         sq_ref[tok_at, :] = (gated * gated).astype(bf16)
         g_ref[tok_at, :] = (gated * gain_ref[...]).astype(bf16)
-        return carry
 
     load_turned.wait()
     load_out.wait()
-    lax.fori_loop(0, requests // many, body, 0)
+    for n in range(requests // many):
+        body(n)
 
     side[2].start()
     side[3].start()
     side[4].start()
 
-    ones = jnp.ones((STAT_ROWS, inner), bf16)
+    ones = jnp.ones((8, inner), bf16)
     squares = lax.dot_general(ones, sq_ref[...], NT, preferred_element_type=f32)
     high = squares.astype(bf16).astype(f32)
     first = lax.broadcasted_iota(jnp.int32, squares.shape, 0) == 0
@@ -305,17 +312,18 @@
 
     for b in range(peers):
         piece = jnp.concatenate(
-            [stats[:, b * pair : (b + 1) * pair], jnp.zeros((STAT_ROWS, 128 - pair), bf16)], axis=1
+            [stats[:STAT_ROWS, b * pair : (b + 1) * pair], jnp.zeros((STAT_ROWS, 128 - pair), bf16)], axis=1
         )
         for h in range(heads_dev):
-            out_ref[b, h, data_rows:, :] = piece
+            out_ref[b, h, data_rows // STAT_ROWS] = piece
 
     for h in range(heads_dev):
         res = jnp.dot(
             g_ref[...], wout_ref[:, h * part : (h + 1) * part], preferred_element_type=f32
         ).astype(bf16)
-        out_ref[:, h, 0:pair, :] = res[:, :128].reshape(peers, pair, 128)
-        out_ref[:, h, pair:data_rows, :] = res[:, 128:].reshape(peers, pair, 128)
+        part_rows = pair // STAT_ROWS
+        out_ref[:, h, :part_rows] = res[:, :128].reshape(peers, part_rows, STAT_ROWS, 128)
+        out_ref[:, h, part_rows : 2 * part_rows] = res[:, 128:].reshape(peers, part_rows, STAT_ROWS, 128)
         leave(h).start()
     for h in range(heads_dev):
         leave(h).wait()
@@ -380,40 +388,44 @@
     lax.fori_loop(0, requests, lambda i, c: (save_state(i).wait(), c)[1], 0)
 
 
-def final_kernel(slot_ref, len_ref, recv_ref, out_ref, seen, *, heads_dev, inner_all):
+def final_kernel(slot_ref, len_ref, recv_ref, out_ref, order, *, heads_dev, inner_all):
     requests, steps, part = out_ref.shape
-    peers = seen.shape[0]
+    peers = requests // 2
     pair = 2 * steps
     data_rows = 2 * pair
     base = lax.axis_index("req") * requests
-    for o in range(peers):
-        seen[o] = 0
-    view = recv_ref.reshape(peers, heads_dev, data_rows + STAT_ROWS, 128)
+
+    def note(i, owner, j):
+        order[owner * 2 + j] = i
+
+    visit(slot_ref, base, requests, note)
+    groups = data_rows // STAT_ROWS
+    view = recv_ref.reshape(peers, heads_dev, groups + 1, STAT_ROWS, 128)
+    own = lax.broadcasted_iota(jnp.int32, (pair, 128), 0) == lax.broadcasted_iota(
+        jnp.int32, (pair, 128), 1
+    )
     place = lax.broadcasted_iota(jnp.int32, (steps, 128), 0)
-    lane = lax.broadcasted_iota(jnp.int32, (steps, 128), 1)
-
-    def body(i, carry):
-        owner = lax.div(slot_ref[base + i], requests)
-        length = len_ref[base + i]
-        j = seen[owner]
-        seen[owner] = j + 1
-        stats = view[owner, 0, data_rows:, :].astype(f32)
+
+    def body(o, carry):
+        stats = view[o, 0, groups].astype(f32)
+        acc = view[o, 0, :groups].astype(f32)
         for h in range(1, heads_dev):
-            stats = stats + view[owner, h, data_rows:, :].astype(f32)
+            stats = stats + view[o, h, groups].astype(f32)
+            acc = acc + view[o, h, :groups].astype(f32)
+        acc = acc.reshape(data_rows, 128)
         squares = stats[0:1, :] + stats[1:2, :]
-        total = jnp.sum(jnp.where(lane == place + j * steps, squares, 0.0), axis=1, keepdims=True)
-        scale = jnp.where(place < length, lax.rsqrt(total / inner_all + 1e-05), 0.0)
-        for half in range(2):
-            rows = pl.ds(pl.multiple_of(half * pair + j * steps, steps), steps)
-            acc = view[owner, 0, rows, :].astype(f32)
-            for h in range(1, heads_dev):
-                acc = acc + view[owner, h, rows, :].astype(f32)
-            out_ref[i, :, half * 128 : (half + 1) * 128] = jnp.where(
-                place < length, acc * scale, 0.0
-            ).astype(bf16)
+        total = jnp.sum(jnp.where(own, squares, 0.0), axis=1, keepdims=True)
+        scale = lax.rsqrt(total / inner_all + 1e-05)
+        for j in range(2):
+            i = order[o * 2 + j]
+            keep = place < len_ref[base + i]
+            for half in range(2):
+                at = half * pair + j * steps
+                value = acc[at : at + steps, :] * scale[j * steps : (j + 1) * steps, :]
+                out_ref[i, :, half * 128 : (half + 1) * 128] = jnp.where(keep, value, 0.0).astype(bf16)
         return carry
 
-    lax.fori_loop(0, requests, body, 0, unroll=4)
+    lax.fori_loop(0, peers, body, 0, unroll=4)
 
 
 def vmem(n):
@@ -463,7 +475,7 @@
     heads_dev = lax.axis_size("head")
     tokens = requests * steps
     spread = heads * steps
-    out_rows = 4 * steps + STAT_ROWS
+    out_rows = 4 * steps // STAT_ROWS + 1
     me = lax.axis_index("req")
 
     slot_blocks = slot.reshape(peers, requests)
@@ -474,8 +486,6 @@
         out_specs=hbm(1)[0],
         scratch_shapes=[
             pltpu.VMEM((peers * heads_dev * 2, steps, part), bf16),
-            pltpu.SMEM((peers,), jnp.int32),
-            pltpu.SMEM((requests,), jnp.int32),
             pltpu.SemaphoreType.DMA((peers,)),
         ],
         compiler_params=pltpu.CompilerParams(vmem_limit_bytes=4 * MIB),
@@ -514,7 +524,7 @@
     leaving, push, b_conv, decay, x_in, bc_in = pl.pallas_call(
         functools.partial(mix_kernel, heads_dev=heads_dev),
         out_shape=(
-            pltpu.HBM((peers, heads_dev, out_rows, 128), bf16),
+            pltpu.HBM((peers, heads_dev, out_rows, STAT_ROWS, 128), bf16),
             pltpu.HBM((requests, steps, inner), bf16),
             pltpu.HBM((requests, steps, nstate), bf16),
             pltpu.HBM((requests, 1, heads), f32),
@@ -532,7 +542,7 @@
             pltpu.VMEM((requests, steps, spread), f32),
             pltpu.VMEM((tokens, inner), bf16),
             pltpu.VMEM((tokens, inner), bf16),
-            pltpu.VMEM((peers, heads_dev, out_rows, 128), bf16),
+            pltpu.VMEM((peers, heads_dev, out_rows, STAT_ROWS, 128), bf16),
             pltpu.VMEM((requests, steps, inner), bf16),
             pltpu.VMEM((requests, steps, nstate), bf16),
             pltpu.VMEM((requests, steps, inner), bf16),
@@ -544,7 +554,7 @@
             pltpu.VMEM((requests, 1, heads), f32),
             pltpu.SemaphoreType.DMA((heads_dev,)),
             pltpu.SemaphoreType.DMA((5,)),
-            pltpu.SemaphoreType.DMA((4,)),
+            pltpu.SemaphoreType.DMA((5,)),
         ],
         compiler_params=pltpu.CompilerParams(vmem_limit_bytes=MIX_MIB * MIB),
         cost_estimate=pl.CostEstimate(flops=4 * 10**9, bytes_accessed=8 * MIB, transcendentals=10**6),
@@ -567,7 +577,7 @@
         in_hbm(w_out),
         in_hbm(turned),
     )
-    leaving = leaving.reshape(peers * heads_dev, out_rows, 128)
+    leaving = leaving.reshape(peers * heads_dev, out_rows, STAT_ROWS, 128)
     returned = lax.all_to_all(leaving, ("req", "head"), split_axis=0, concat_axis=0, tiled=True)
     new_state, new_conv_x, new_conv_bc = pl.pallas_call(
         state_kernel,
@@ -594,7 +604,7 @@
         out_shape=jax.ShapeDtypeStruct((requests, steps, part), bf16),
         in_specs=[smem(), smem()] + vmem(1),
         out_specs=vmem(1)[0],
-        scratch_shapes=[pltpu.SMEM((peers,), jnp.int32)],
+        scratch_shapes=[pltpu.SMEM((requests,), jnp.int32)],
         compiler_params=pltpu.CompilerParams(vmem_limit_bytes=4 * MIB),
         name="place_rows",
     )(slot, lengths, returned)

time: 98.9 us -> 96.4 us (0.975)
  Pallas kernels: 37.1 us -> 35.9 us
  transfers between devices with their start and end apart: 2 -> 2, of which waited for: 2 -> 2; matrix products, arithmetic and copies ran while one was open for 8% -> 8% of each run, Pallas kernels for 19% -> 20%
where the time goes in v3:
time: 96.4 us; the launch traced here: 96 us
  Pallas kernels  35.9 us (37%)
  waiting for transfers between devices  32.8 us (34%)
  starting transfers between devices  16.3 us (17%)
  local copies, waits for them, and re-layouts  9.84 us (10%)
    all_to_all x1, waiting for transfers between devices, per_device(): lax.all_to_all(outgoing, ('req', 'head'), split_axis=0, concat_axis=0, ti...  17.1 us
    all_to_all x1, waiting for transfers between devices, per_device(): lax.all_to_all(leaving, ('req', 'head'), split_axis=0, concat_axis=0, til...  15.7 us
    pallas_call x1, Pallas kernels, per_device(): pl.pallas_call(state_kernel, out_shape=(pltpu.HBM((requests, inner, nstat...  12.8 us
    pallas_call x1, Pallas kernels, per_device(): pl.pallas_call(functools.partial(mix_kernel, heads_dev=heads_dev), out_sh...  12.1 us
    all_to_all x1, starting transfers between devices, per_device(): lax.all_to_all(outgoing, ('req', 'head'), split_axis=0, concat_axis=0, ti...  11.5 us
    unnamed x40, local copies, waits for them, and re-layouts  9.09 us
    pallas_call x1, Pallas kernels, per_device(): pl.pallas_call(stage_kernel, out_shape=pltpu.HBM((requests, nstate, inner...  6.26 us
    all_to_all x1, starting transfers between devices, per_device(): lax.all_to_all(leaving, ('req', 'head'), split_axis=0, concat_axis=0, til...  4.76 us
  transfers between devices with their start and end apart: 2, of which 2 were waited for; matrix products, arithmetic and copies ran while one was open for 8% of the time, Pallas kernels for 20%

profile of v3, /device:TPU:1, one launch (start us, length us, event | category | flops | bytes accessed | tf_op | source)
XLA Modules:
  0.0 96.0 jit_solution(405825084536554375)
XLA Ops:
  0.7 2.6 %send_rows.1 = bf16[256,16,256]{2,1,0:T(8,128)(2,1)} custom-call(s32[512]{0:T(512)} %slot_ref.3, bf16[32,16,256]{2,1,0:T(8,128)(2,1)} %hid_ref.1), custom_call_target="tpu_custom_call" | custom-call | tf_op jit(solution)/shard_map/send_rows/pallas_call | solution.py:482
  3.4 11.5 %all-to-all-start = ((bf16[256,16,256]{2,1,0:T(8,128)(2,1)}), bf16[256,16,256]{2,1,0:T(8,128)(2,1)S(1)}, u32[]{:S(2)}, u32[]{:S(2)}) async-start(bf16[256,16,256]{2,1,0:T(8,128)(2,1)} %send_rows.1), calls=%async_computation | async-start | bytes 4194304 | tf_op jit(solution)/shard_map/all_to_all | solution.py:494
  14.9 0.1 reshape.57
  15.0 0.1 broadcast_in_dim.31
  15.0 0.1 broadcast_in_dim_reshape.3.skip_ref
  15.1 0.1 reshape.58
  15.2 0.1 select_reduce_fusion.1
  15.4 0.1 copy.37
  15.4 0.1 reshape.59
  15.6 0.1 broadcast_in_dim.33
  15.6 0.1 broadcast_in_dim.34
  15.7 0.1 copy.40.cb_ref
  15.8 0.1 copy.39.cx_ref
  16.0 0.3 copy.38.wdt_ref
  16.2 5.4 %copy.45 = bf16[256,8,2,512]{3,1,2,0:T(8,128)(2,1)} copy(bf16[256,8,2,512]{3,2,1,0:T(2,128)(2,1)} %bitcast.16) | data formatting | bytes 8388608
  21.6 0.1 pad_add_fusion.1.arrive
  21.7 0.0 copy-start.11
  21.7 6.3 %stage.1.turned_hbm = bf16[32,128,512]{2,1,0:T(8,128)(2,1)} custom-call(s32[64]{0:T(128)S(1)} %pad_add_fusion.1.arrive, f32[32,512,128]{2,1,0:T(8,128)} %bitcast.13), custom_call_target="tpu_custom_call" | custom-call | flops 1000000000 | bytes 20971520 | tf_op jit(solution)/shard_map/stage/pallas_call | solution.py:509
  28.0 17.1 %all-to-all-done.recv_ref = bf16[256,16,256]{2,1,0:T(8,128)(2,1)S(1)} async-done(((bf16[256,16,256]{2,1,0:T(8,128)(2,1)}), bf16[256,16,256]{2,1,0:T(8,128)(2,1)S(1)}, u32[]{:S(2)}, u32[]{:S(2)}) %all-to-all-start) | async-done | bytes 2097184 | tf_op jit(solution)/shard_map/all_to_all | solution.py:494
  45.0 0.1 broadcast_in_dim.35.cvec_ref
  45.2 12.1 %mix.1 = (bf16[16,8,17,4,128]{4,3,2,1,0:T(4,128)(2,1)}, bf16[32,16,512]{2,1,0:T(8,128)(2,1)}, bf16[32,16,128]{2,1,0:T(8,128)(2,1)}, f32[32,1,8]{2,1,0:T(1,128)},...) custom-call(s32[64]{0:T(128)S(1)} %pad_add_fusion.1.arrive, bf16[256,16,256]{2,1,0:T(8,128)(2,1)S(1)} %all-to-all-done.recv_ref, ...), custom_call_target="tpu_custom_call" | custom-call | flops 4000000000 | bytes 8388608 | tf_op jit(solution)/shard_map/mix/pallas_call | solution.py:524
  57.3 0.0 copy-start
  57.3 0.0 copy-start.2
  57.3 0.0 copy-start.3
  57.3 4.8 %all-to-all-start.1 = ((bf16[128,17,4,128]{3,2,1,0:T(4,128)(2,1)}), bf16[128,17,4,128]{3,2,1,0:T(4,128)(2,1)S(1)}, u32[]{:S(2)}, u32[]{:S(2)}) async-start(bf16[128,17,4,128]{3,2,1,0:T(4,128)(2,1)} %bitcast.17), calls=%async_computation.1 | async-start | bytes 4456448 | tf_op jit(solution)/shard_map/all_to_all | solution.py:581
  62.1 1.0 %copy-done.1 = bf16[32,16,512]{2,1,0:T(8,128)(2,1)S(1)} copy-done((bf16[32,16,512]{2,1,0:T(8,128)(2,1)S(1)}, bf16[32,16,512]{2,1,0:T(8,128)(2,1)}, u32[]{:S(2)}) %copy-start.1) | copy-done | bytes 524312
  63.2 0.7 copy-done.5
  63.9 12.8 %update.1 = (f32[32,512,128]{2,1,0:T(8,128)}, f32[32,3,512]{2,1,0:T(4,128)S(1)}, f32[32,3,256]{2,1,0:T(4,128)S(1)}) custom-call(s32[64]{0:T(128)S(1)} %pad_add_fusion.1.arrive, bf16[32,16,512]{2,1,0:T(8,128)(2,1)S(1)} %copy-done, bf16[32,16,128]{2,1,0:T(8,128)(2,1)S(1)} %copy-done.3, f32[32,1,8]{2,1,0:T(1,128)S(1)} %copy-done.5, ...), custom_call_target="tpu_custom_call" | custom-call | flops 2000000000 | bytes 20971520 | tf_op jit(solution)/shard_map/update/pallas_call | solution.py:582
  76.7 0.7 copy.44
  77.3 0.7 copy.43
  78.1 15.7 %all-to-all-done.1.recv_ref = bf16[128,17,4,128]{3,2,1,0:T(4,128)(2,1)S(1)} async-done(((bf16[128,17,4,128]{3,2,1,0:T(4,128)(2,1)}), bf16[128,17,4,128]{3,2,1,0:T(4,128)(2,1)S(1)}, u32[]{:S(2)}, u32[]{:S(2)}) %all-to-all-start.1) | async-done | bytes 2228256 | tf_op jit(solution)/shard_map/all_to_all | solution.py:581
  93.8 2.2 %place_rows.1 = bf16[32,16,256]{2,1,0:T(8,128)(2,1)} custom-call(s32[512]{0:T(512)S(1)} %copy-done.4, s32[512]{0:T(512)S(1)} %copy-done.8, bf16[128,17,4,128]{3,2,1,0:T(4,128)(2,1)S(1)} %all-to-all-done.1.recv_ref), custom_call_target="tpu_custom_call" | custom-call | tf_op jit(solution)/shard_map/place_rows/pallas_call | solution.py:602
  (32 shorter events, 0.1 us)
Async XLA Ops:
  0.6 14.2 %copy-start.4 = (s32[512]{0:T(512)S(1)}, s32[512]{0:T(512)}, u32[]{:S(2)}) copy-start(s32[512]{0:T(512)} %slot_ref.3) | copy-start | bytes 6148
  0.6 14.3 %copy-start.16 = (f32[8]{0:T(128)S(1)}, f32[8]{0:T(128)}, u32[]{:S(2)}) copy-start(f32[8]{0:T(128)} %param.25) | copy-start | bytes 100
  0.7 14.5 %copy-start.8 = (s32[512]{0:T(512)S(1)}, s32[512]{0:T(512)}, u32[]{:S(2)}) copy-start(s32[512]{0:T(512)} %len_ref.1) | copy-start | bytes 6148
  0.7 14.5 %copy-start.15 = (s32[512]{0:T(512)S(1)}, s32[512]{0:T(512)}, u32[]{:S(2)}) copy-start(s32[512]{0:T(512)} %param.33) | copy-start | bytes 6148
  0.7 15.0 %copy-start.13 = (f32[32,3,256]{2,0,1:T(8,128)S(1)}, f32[32,3,256]{2,0,1:T(8,128)}, u32[]{:S(2)}) copy-start(f32[32,3,256]{2,0,1:T(8,128)} %param.30) | copy-start | bytes 294916
  0.7 15.1 %copy-start.12 = (f32[32,3,512]{2,0,1:T(8,128)S(1)}, f32[32,3,512]{2,0,1:T(8,128)}, u32[]{:S(2)}) copy-start(f32[32,3,512]{2,0,1:T(8,128)} %param.29) | copy-start | bytes 589828
  0.7 15.2 %copy-start.14 = (bf16[2048,8]{0,1:T(8,128)(2,1)S(1)}, bf16[2048,8]{0,1:T(8,128)(2,1)}, u32[]{:S(2)}) copy-start(bf16[2048,8]{0,1:T(8,128)(2,1)} %param.20) | copy-start | bytes 98308
  3.4 41.7 %all-to-all-start = ((bf16[256,16,256]{2,1,0:T(8,128)(2,1)}), bf16[256,16,256]{2,1,0:T(8,128)(2,1)S(1)}, u32[]{:S(2)}, u32[]{:S(2)}) async-start(bf16[256,16,256]{2,1,0:T(8,128)(2,1)} %send_rows.1), calls=%async_computation | async-start | bytes 4194304 | tf_op jit(solution)/shard_map/all_to_all | solution.py:494
  21.7 23.5 %copy-start.6 = (f32[5,512]{1,0:T(8,128)S(1)}, f32[5,512]{1,0:T(8,128)}, u32[]{:S(2)}) copy-start(f32[5,512]{1,0:T(8,128)} %cxw_ref.1) | copy-start | bytes 30724
  21.7 23.5 %copy-start.7 = (f32[5,256]{1,0:T(8,128)S(1)}, f32[5,256]{1,0:T(8,128)}, u32[]{:S(2)}) copy-start(f32[5,256]{1,0:T(8,128)} %cbw_ref.1) | copy-start | bytes 15364
  21.7 23.5 %copy-start.9 = (f32[512]{0:T(512)S(1)}, f32[512]{0:T(512)}, u32[]{:S(2)}) copy-start(f32[512]{0:T(512)} %param.26) | copy-start | bytes 6148
  21.7 23.5 %copy-start.10 = (f32[8]{0:T(128)S(1)}, f32[8]{0:T(128)}, u32[]{:S(2)}) copy-start(f32[8]{0:T(128)} %param.23) | copy-start | bytes 100
  21.7 23.5 %copy-start.11 = (f32[8]{0:T(128)S(1)}, f32[8]{0:T(128)}, u32[]{:S(2)}) copy-start(f32[8]{0:T(128)} %param.24) | copy-start | bytes 100
  57.3 4.8 %copy-start = (bf16[32,16,512]{2,1,0:T(8,128)(2,1)S(1)}, bf16[32,16,512]{2,1,0:T(8,128)(2,1)}, u32[]{:S(2)}) copy-start(bf16[32,16,512]{2,1,0:T(8,128)(2,1)} %get-tuple-element.14.push_ref) | copy-start | bytes 1572868
  57.3 4.8 %copy-start.2 = (bf16[32,16,256]{2,1,0:T(8,128)(2,1)S(1)}, bf16[32,16,256]{2,1,0:T(8,128)(2,1)}, u32[]{:S(2)}) copy-start(bf16[32,16,256]{2,1,0:T(8,128)(2,1)} %get-tuple-element.18.bin_ref) | copy-start | bytes 786436
  57.3 4.8 %copy-start.3 = (bf16[32,16,128]{2,1,0:T(8,128)(2,1)S(1)}, bf16[32,16,128]{2,1,0:T(8,128)(2,1)}, u32[]{:S(2)}) copy-start(bf16[32,16,128]{2,1,0:T(8,128)(2,1)} %get-tuple-element.15.b_ref) | copy-start | bytes 393220
  57.3 36.5 %all-to-all-start.1 = ((bf16[128,17,4,128]{3,2,1,0:T(4,128)(2,1)}), bf16[128,17,4,128]{3,2,1,0:T(4,128)(2,1)S(1)}, u32[]{:S(2)}, u32[]{:S(2)}) async-start(bf16[128,17,4,128]{3,2,1,0:T(4,128)(2,1)} %bitcast.17), calls=%async_computation.1 | async-start | bytes 4456448 | tf_op jit(solution)/shard_map/all_to_all | solution.py:581
  62.1 1.0 %copy-start.1 = (bf16[32,16,512]{2,1,0:T(8,128)(2,1)S(1)}, bf16[32,16,512]{2,1,0:T(8,128)(2,1)}, u32[]{:S(2)}) copy-start(bf16[32,16,512]{2,1,0:T(8,128)(2,1)} %get-tuple-element.17.xin_ref) | copy-start | bytes 1572868
  63.2 0.7 copy-start.5

commit v4 on v3

--- a/solution.py
+++ b/solution.py
@@ -165,14 +165,65 @@
     lax.fori_loop(0, requests, previous, 0, unroll=4)
 
     view = recv_ref.reshape(peers, heads_dev, 2, steps, part)
-    tok = jnp.concatenate(
-        [view[:, h].reshape(tokens, part) for h in range(heads_dev)], axis=1
-    )
-
     def proj(w):
-        return jnp.dot(tok, w, preferred_element_type=f32).astype(bf16)
+        half = peers // 2
+        return jnp.concatenate(
+            [
+                jnp.dot(
+                    jnp.concatenate(
+                        [
+                            view[k * half : (k + 1) * half, h].reshape(tokens // 2, part)
+                            for h in range(heads_dev)
+                        ],
+                        axis=1,
+                    ),
+                    w,
+                    preferred_element_type=f32,
+                ).astype(bf16)
+                for k in range(2)
+            ],
+            axis=0,
+        )
 
     dt_in = proj(wdt_ref[...]).astype(f32)
+    pre = dt_in + bias_ref[...]
+    dt = jnp.maximum(pre, 0.0) + jnp.log1p(jnp.exp(-jnp.abs(pre)))
+    rate = -dt * jnp.exp(alog_ref[...])
+    place = lax.rem(lax.broadcasted_iota(jnp.int32, (tokens, heads), 0), steps)
+    cumul = rate
+    d = 1
+    while d < steps:
+        cumul = cumul + jnp.where(place >= d, pltpu.roll(cumul, d, 0), 0.0)
+        d *= 2
+    live = place < cvec_ref[...]
+    last = place == cvec_ref[...] - 1
+    total = jnp.sum(jnp.where(last, cumul, 0.0).reshape(requests, steps, heads), axis=1, keepdims=True)
+    dec_ref[...] = jnp.exp(total)
+    totals = jnp.broadcast_to(total, (requests, steps, heads)).reshape(tokens, heads)
+    scaled = jnp.where(live, jnp.exp(jnp.where(live, totals - cumul, 0.0)) * dt, 0.0)
+
+    def widen(x, width, each, terms):
+        rows = lax.broadcasted_iota(jnp.int32, (heads, width), 0)
+        cols = lax.div(lax.broadcasted_iota(jnp.int32, (heads, width), 1), each)
+        pick = (rows == cols).astype(bf16)
+        wide = None
+        for term in split(x, terms):
+            more = jnp.dot(term, pick, preferred_element_type=f32)
+            wide = more if wide is None else wide + more
+        return wide.reshape(requests, steps, width)
+
+    ec_ref[...] = widen(jnp.exp(cumul), inner, headdim, 2)
+    sc_ref[...] = widen(scaled, inner, headdim, 2)
+    cum2 = widen(cumul, spread, steps, 3)
+    dt2 = widen(dt, spread, steps, 2)
+    t_at = lax.broadcasted_iota(jnp.int32, (1, steps, spread), 1)
+    s_at = lax.rem(lax.broadcasted_iota(jnp.int32, (1, steps, spread), 2), steps)
+    same = t_at == s_at
+    lower = t_at >= s_at
+    crow = jnp.sum(jnp.where(same, cum2, 0.0), axis=1, keepdims=True)
+    drow = jnp.sum(jnp.where(same, dt2, 0.0), axis=1, keepdims=True)
+    fd_ref[...] = jnp.where(lower, jnp.exp(jnp.where(lower, cum2 - crow, 0.0)) * drow, 0.0)
+
     load_x.wait()
     load_bc.wait()
     for n in range(blocks):
@@ -196,49 +247,12 @@
     for n in range(blocks):
         gate_ref[:, n * blk : (n + 1) * blk] = proj(wzx_ref[:, n * blk : (n + 1) * blk])
 
-    pre = dt_in + bias_ref[...]
-    dt = jnp.maximum(pre, 0.0) + jnp.log1p(jnp.exp(-jnp.abs(pre)))
-    rate = -dt * jnp.exp(alog_ref[...])
-    place = lax.rem(lax.broadcasted_iota(jnp.int32, (tokens, heads), 0), steps)
-    cumul = rate
-    d = 1
-    while d < steps:
-        cumul = cumul + jnp.where(place >= d, pltpu.roll(cumul, d, 0), 0.0)
-        d *= 2
-    live = place < cvec_ref[...]
-    total = jnp.sum(jnp.where(live, rate, 0.0).reshape(requests, steps, heads), axis=1, keepdims=True)
-    dec_ref[...] = jnp.exp(total)
-    totals = jnp.broadcast_to(total, (requests, steps, heads)).reshape(tokens, heads)
-    scaled = jnp.where(live, jnp.exp(jnp.where(live, totals - cumul, 0.0)) * dt, 0.0)
-
-    def widen(x, width, each, terms):
-        rows = lax.broadcasted_iota(jnp.int32, (heads, width), 0)
-        cols = lax.div(lax.broadcasted_iota(jnp.int32, (heads, width), 1), each)
-        pick = (rows == cols).astype(bf16)
-        wide = None
-        for term in split(x, terms):
-            more = jnp.dot(term, pick, preferred_element_type=f32)
-            wide = more if wide is None else wide + more
-        return wide.reshape(requests, steps, width)
-
-    ec_ref[...] = widen(jnp.exp(cumul), inner, headdim, 2)
-    sc_ref[...] = widen(scaled, inner, headdim, 2)
-    cum2 = widen(cumul, spread, steps, 3)
-    dt2 = widen(dt, spread, steps, 2)
-    t_at = lax.broadcasted_iota(jnp.int32, (1, steps, spread), 1)
-    s_at = lax.rem(lax.broadcasted_iota(jnp.int32, (1, steps, spread), 2), steps)
-    same = t_at == s_at
-    lower = t_at >= s_at
-    crow = jnp.sum(jnp.where(same, cum2, 0.0), axis=1, keepdims=True)
-    drow = jnp.sum(jnp.where(same, dt2, 0.0), axis=1, keepdims=True)
-    fd_ref[...] = jnp.where(lower, jnp.exp(jnp.where(lower, cum2 - crow, 0.0)) * drow, 0.0)
-
     group = heads // 2
     gspread, ginner = group * steps, group * headdim
     r_head = lax.div(lax.broadcasted_iota(jnp.int32, (gspread, ginner), 0), steps)
     c_head = lax.div(lax.broadcasted_iota(jnp.int32, (gspread, ginner), 1), headdim)
     diag = (r_head == c_head).astype(bf16)
-    many = 8
+    many = 16
     rows = many * steps
     own = lax.div(lax.broadcasted_iota(jnp.int32, (rows, rows), 0), steps) == lax.div(
         lax.broadcasted_iota(jnp.int32, (rows, rows), 1), steps
@@ -318,9 +332,16 @@
             out_ref[b, h, data_rows // STAT_ROWS] = piece
 
     for h in range(heads_dev):
-        res = jnp.dot(
-            g_ref[...], wout_ref[:, h * part : (h + 1) * part], preferred_element_type=f32
-        ).astype(bf16)
+        cols = wout_ref[:, h * part : (h + 1) * part]
+        res = jnp.concatenate(
+            [
+                jnp.dot(
+                    g_ref[k * tokens // 2 : (k + 1) * tokens // 2, :], cols, preferred_element_type=f32
+                ).astype(bf16)
+                for k in range(2)
+            ],
+            axis=0,
+        )
         part_rows = pair // STAT_ROWS
         out_ref[:, h, :part_rows] = res[:, :128].reshape(peers, part_rows, STAT_ROWS, 128)
         out_ref[:, h, part_rows : 2 * part_rows] = res[:, 128:].reshape(peers, part_rows, STAT_ROWS, 128)

time: 96.4 us -> 94.8 us (0.983)
  Pallas kernels: 35.9 us -> 34.3 us
    pallas_call x1, Pallas kernels: 12.1 us -> 10.5 us  [per_device(): pl.pallas_call(functools.partial(mix_kernel, heads_dev=heads_dev), out_sh...]
  transfers between devices with their start and end apart: 2 -> 2, of which waited for: 2 -> 2; matrix products, arithmetic and copies ran while one was open for 8% -> 9% of each run, Pallas kernels for 20% -> 20%
where the time goes in v4:
time: 94.8 us; the launch traced here: 94.4 us
  Pallas kernels  34.3 us (36%)
  waiting for transfers between devices  32.8 us (35%)
  starting transfers between devices  16.3 us (17%)
  local copies, waits for them, and re-layouts  9.84 us (10%)
    all_to_all x1, waiting for transfers between devices, per_device(): lax.all_to_all(outgoing, ('req', 'head'), split_axis=0, concat_axis=0, ti...  17.1 us
    all_to_all x1, waiting for transfers between devices, per_device(): lax.all_to_all(leaving, ('req', 'head'), split_axis=0, concat_axis=0, til...  15.7 us
    pallas_call x1, Pallas kernels, per_device(): pl.pallas_call(state_kernel, out_shape=(pltpu.HBM((requests, inner, nstat...  12.8 us
    all_to_all x1, starting transfers between devices, per_device(): lax.all_to_all(outgoing, ('req', 'head'), split_axis=0, concat_axis=0, ti...  11.5 us
    pallas_call x1, Pallas kernels, per_device(): pl.pallas_call(functools.partial(mix_kernel, heads_dev=heads_dev), out_sh...  10.5 us
    unnamed x40, local copies, waits for them, and re-layouts  9.09 us
    pallas_call x1, Pallas kernels, per_device(): pl.pallas_call(stage_kernel, out_shape=pltpu.HBM((requests, nstate, inner...  6.26 us
    all_to_all x1, starting transfers between devices, per_device(): lax.all_to_all(leaving, ('req', 'head'), split_axis=0, concat_axis=0, til...  4.75 us
  transfers between devices with their start and end apart: 2, of which 2 were waited for; matrix products, arithmetic and copies ran while one was open for 9% of the time, Pallas kernels for 20%

profile of v4, /device:TPU:1, one launch (start us, length us, event | category | flops | bytes accessed | tf_op | source)
XLA Modules:
  0.0 94.4 jit_solution(7964300735983205547)
XLA Ops:
  0.7 2.6 %send_rows.1 = bf16[256,16,256]{2,1,0:T(8,128)(2,1)} custom-call(s32[512]{0:T(512)} %slot_ref.3, bf16[32,16,256]{2,1,0:T(8,128)(2,1)} %hid_ref.1), custom_call_target="tpu_custom_call" | custom-call | tf_op jit(solution)/shard_map/send_rows/pallas_call | solution.py:503
  3.3 11.5 %all-to-all-start = ((bf16[256,16,256]{2,1,0:T(8,128)(2,1)}), bf16[256,16,256]{2,1,0:T(8,128)(2,1)S(1)}, u32[]{:S(2)}, u32[]{:S(2)}) async-start(bf16[256,16,256]{2,1,0:T(8,128)(2,1)} %send_rows.1), calls=%async_computation | async-start | bytes 4194304 | tf_op jit(solution)/shard_map/all_to_all | solution.py:515
  14.8 0.1 reshape.57
  14.9 0.1 broadcast_in_dim.31
  15.0 0.1 broadcast_in_dim_reshape.3.skip_ref
  15.1 0.0 copy-done.15
  15.1 0.1 reshape.58
  15.2 0.1 select_reduce_fusion.1
  15.3 0.1 copy.37
  15.4 0.1 reshape.59
  15.5 0.1 broadcast_in_dim.33
  15.6 0.1 broadcast_in_dim.34
  15.7 0.1 copy.40.cb_ref
  15.7 0.1 copy.39.cx_ref
  15.9 0.3 copy.38.wdt_ref
  16.2 5.4 %copy.45 = bf16[256,8,2,512]{3,1,2,0:T(8,128)(2,1)} copy(bf16[256,8,2,512]{3,2,1,0:T(2,128)(2,1)} %bitcast.16) | data formatting | bytes 8388608
  21.6 0.1 pad_add_fusion.1.arrive
  21.7 0.0 copy-start.11
  21.7 6.3 %stage.1.turned_hbm = bf16[32,128,512]{2,1,0:T(8,128)(2,1)} custom-call(s32[64]{0:T(128)S(1)} %pad_add_fusion.1.arrive, f32[32,512,128]{2,1,0:T(8,128)} %bitcast.13), custom_call_target="tpu_custom_call" | custom-call | flops 1000000000 | bytes 20971520 | tf_op jit(solution)/shard_map/stage/pallas_call | solution.py:530
  27.9 17.1 %all-to-all-done.recv_ref = bf16[256,16,256]{2,1,0:T(8,128)(2,1)S(1)} async-done(((bf16[256,16,256]{2,1,0:T(8,128)(2,1)}), bf16[256,16,256]{2,1,0:T(8,128)(2,1)S(1)}, u32[]{:S(2)}, u32[]{:S(2)}) %all-to-all-start) | async-done | bytes 2097184 | tf_op jit(solution)/shard_map/all_to_all | solution.py:515
  45.0 0.1 broadcast_in_dim.35.cvec_ref
  45.2 10.5 %mix.1 = (bf16[16,8,17,4,128]{4,3,2,1,0:T(4,128)(2,1)}, bf16[32,16,512]{2,1,0:T(8,128)(2,1)}, bf16[32,16,128]{2,1,0:T(8,128)(2,1)}, f32[32,1,8]{2,1,0:T(1,128)},...) custom-call(s32[64]{0:T(128)S(1)} %pad_add_fusion.1.arrive, bf16[256,16,256]{2,1,0:T(8,128)(2,1)S(1)} %all-to-all-done.recv_ref, ...), custom_call_target="tpu_custom_call" | custom-call | flops 4000000000 | bytes 8388608 | tf_op jit(solution)/shard_map/mix/pallas_call | solution.py:545
  55.7 0.0 copy-start.2
  55.7 0.0 copy-start.3
  55.7 4.7 %all-to-all-start.1 = ((bf16[128,17,4,128]{3,2,1,0:T(4,128)(2,1)}), bf16[128,17,4,128]{3,2,1,0:T(4,128)(2,1)S(1)}, u32[]{:S(2)}, u32[]{:S(2)}) async-start(bf16[128,17,4,128]{3,2,1,0:T(4,128)(2,1)} %bitcast.17), calls=%async_computation.1 | async-start | bytes 4456448 | tf_op jit(solution)/shard_map/all_to_all | solution.py:602
  60.5 1.0 %copy-done.1 = bf16[32,16,512]{2,1,0:T(8,128)(2,1)S(1)} copy-done((bf16[32,16,512]{2,1,0:T(8,128)(2,1)S(1)}, bf16[32,16,512]{2,1,0:T(8,128)(2,1)}, u32[]{:S(2)}) %copy-start.1) | copy-done | bytes 524312
  61.5 0.7 copy-done.5
  62.2 12.8 %update.1 = (f32[32,512,128]{2,1,0:T(8,128)}, f32[32,3,512]{2,1,0:T(4,128)S(1)}, f32[32,3,256]{2,1,0:T(4,128)S(1)}) custom-call(s32[64]{0:T(128)S(1)} %pad_add_fusion.1.arrive, bf16[32,16,512]{2,1,0:T(8,128)(2,1)S(1)} %copy-done, bf16[32,16,128]{2,1,0:T(8,128)(2,1)S(1)} %copy-done.3, f32[32,1,8]{2,1,0:T(1,128)S(1)} %copy-done.5, ...), custom_call_target="tpu_custom_call" | custom-call | flops 2000000000 | bytes 20971520 | tf_op jit(solution)/shard_map/update/pallas_call | solution.py:603
  75.0 0.7 copy.44
  75.7 0.7 copy.43
  76.4 15.7 %all-to-all-done.1.recv_ref = bf16[128,17,4,128]{3,2,1,0:T(4,128)(2,1)S(1)} async-done(((bf16[128,17,4,128]{3,2,1,0:T(4,128)(2,1)}), bf16[128,17,4,128]{3,2,1,0:T(4,128)(2,1)S(1)}, u32[]{:S(2)}, u32[]{:S(2)}) %all-to-all-start.1) | async-done | bytes 2228256 | tf_op jit(solution)/shard_map/all_to_all | solution.py:602
  92.2 2.2 %place_rows.1 = bf16[32,16,256]{2,1,0:T(8,128)(2,1)} custom-call(s32[512]{0:T(512)S(1)} %copy-done.4, s32[512]{0:T(512)S(1)} %copy-done.8, bf16[128,17,4,128]{3,2,1,0:T(4,128)(2,1)S(1)} %all-to-all-done.1.recv_ref), custom_call_target="tpu_custom_call" | custom-call | tf_op jit(solution)/shard_map/place_rows/pallas_call | solution.py:623
  (32 shorter events, 0.1 us)
Async XLA Ops:
  0.6 14.2 %copy-start.4 = (s32[512]{0:T(512)S(1)}, s32[512]{0:T(512)}, u32[]{:S(2)}) copy-start(s32[512]{0:T(512)} %slot_ref.3) | copy-start | bytes 6148
  0.6 14.3 %copy-start.16 = (f32[8]{0:T(128)S(1)}, f32[8]{0:T(128)}, u32[]{:S(2)}) copy-start(f32[8]{0:T(128)} %param.25) | copy-start | bytes 100
  0.7 14.4 %copy-start.8 = (s32[512]{0:T(512)S(1)}, s32[512]{0:T(512)}, u32[]{:S(2)}) copy-start(s32[512]{0:T(512)} %len_ref.1) | copy-start | bytes 6148
  0.7 14.4 %copy-start.15 = (s32[512]{0:T(512)S(1)}, s32[512]{0:T(512)}, u32[]{:S(2)}) copy-start(s32[512]{0:T(512)} %param.33) | copy-start | bytes 6148
  0.7 15.0 %copy-start.13 = (f32[32,3,256]{2,0,1:T(8,128)S(1)}, f32[32,3,256]{2,0,1:T(8,128)}, u32[]{:S(2)}) copy-start(f32[32,3,256]{2,0,1:T(8,128)} %param.30) | copy-start | bytes 294916
  0.7 15.1 %copy-start.12 = (f32[32,3,512]{2,0,1:T(8,128)S(1)}, f32[32,3,512]{2,0,1:T(8,128)}, u32[]{:S(2)}) copy-start(f32[32,3,512]{2,0,1:T(8,128)} %param.29) | copy-start | bytes 589828
  0.7 15.2 %copy-start.14 = (bf16[2048,8]{0,1:T(8,128)(2,1)S(1)}, bf16[2048,8]{0,1:T(8,128)(2,1)}, u32[]{:S(2)}) copy-start(bf16[2048,8]{0,1:T(8,128)(2,1)} %param.20) | copy-start | bytes 98308
  3.3 41.7 %all-to-all-start = ((bf16[256,16,256]{2,1,0:T(8,128)(2,1)}), bf16[256,16,256]{2,1,0:T(8,128)(2,1)S(1)}, u32[]{:S(2)}, u32[]{:S(2)}) async-start(bf16[256,16,256]{2,1,0:T(8,128)(2,1)} %send_rows.1), calls=%async_computation | async-start | bytes 4194304 | tf_op jit(solution)/shard_map/all_to_all | solution.py:515
  21.6 23.5 %copy-start.6 = (f32[5,512]{1,0:T(8,128)S(1)}, f32[5,512]{1,0:T(8,128)}, u32[]{:S(2)}) copy-start(f32[5,512]{1,0:T(8,128)} %cxw_ref.1) | copy-start | bytes 30724
  21.6 23.5 %copy-start.7 = (f32[5,256]{1,0:T(8,128)S(1)}, f32[5,256]{1,0:T(8,128)}, u32[]{:S(2)}) copy-start(f32[5,256]{1,0:T(8,128)} %cbw_ref.1) | copy-start | bytes 15364
  21.7 23.5 %copy-start.9 = (f32[512]{0:T(512)S(1)}, f32[512]{0:T(512)}, u32[]{:S(2)}) copy-start(f32[512]{0:T(512)} %param.26) | copy-start | bytes 6148
  21.7 23.5 %copy-start.10 = (f32[8]{0:T(128)S(1)}, f32[8]{0:T(128)}, u32[]{:S(2)}) copy-start(f32[8]{0:T(128)} %param.23) | copy-start | bytes 100
  21.7 23.5 %copy-start.11 = (f32[8]{0:T(128)S(1)}, f32[8]{0:T(128)}, u32[]{:S(2)}) copy-start(f32[8]{0:T(128)} %param.24) | copy-start | bytes 100
  55.7 4.8 %copy-start = (bf16[32,16,512]{2,1,0:T(8,128)(2,1)S(1)}, bf16[32,16,512]{2,1,0:T(8,128)(2,1)}, u32[]{:S(2)}) copy-start(bf16[32,16,512]{2,1,0:T(8,128)(2,1)} %get-tuple-element.14.push_ref) | copy-start | bytes 1572868
  55.7 4.8 %copy-start.2 = (bf16[32,16,256]{2,1,0:T(8,128)(2,1)S(1)}, bf16[32,16,256]{2,1,0:T(8,128)(2,1)}, u32[]{:S(2)}) copy-start(bf16[32,16,256]{2,1,0:T(8,128)(2,1)} %get-tuple-element.18.bin_ref) | copy-start | bytes 786436
  55.7 4.8 %copy-start.3 = (bf16[32,16,128]{2,1,0:T(8,128)(2,1)S(1)}, bf16[32,16,128]{2,1,0:T(8,128)(2,1)}, u32[]{:S(2)}) copy-start(bf16[32,16,128]{2,1,0:T(8,128)(2,1)} %get-tuple-element.15.b_ref) | copy-start | bytes 393220
  55.7 36.5 %all-to-all-start.1 = ((bf16[128,17,4,128]{3,2,1,0:T(4,128)(2,1)}), bf16[128,17,4,128]{3,2,1,0:T(4,128)(2,1)S(1)}, u32[]{:S(2)}, u32[]{:S(2)}) async-start(bf16[128,17,4,128]{3,2,1,0:T(4,128)(2,1)} %bitcast.17), calls=%async_computation.1 | async-start | bytes 4456448 | tf_op jit(solution)/shard_map/all_to_all | solution.py:602
  60.5 1.0 %copy-start.1 = (bf16[32,16,512]{2,1,0:T(8,128)(2,1)S(1)}, bf16[32,16,512]{2,1,0:T(8,128)(2,1)}, u32[]{:S(2)}) copy-start(bf16[32,16,512]{2,1,0:T(8,128)(2,1)} %get-tuple-element.17.xin_ref) | copy-start | bytes 1572868
  61.5 0.7 copy-start.5

commit v5 on v4

--- a/solution.py
+++ b/solution.py
@@ -88,7 +88,6 @@
     alog_ref,
     skip_ref,
     gain_ref,
-    cvec_ref,
     cx_ref,
     cb_ref,
     wzx_hbm,
@@ -119,6 +118,7 @@
     wout_ref,
     turned_ref,
     dec_ref,
+    cvec_ref,
     out_sem,
     side_sem,
     weight_sem,
@@ -160,6 +160,8 @@
         row = arrive[i]
         xw_ref[i, base:8, :] = cx_ref[row]
         bw_ref[i, base:8, :] = cb_ref[row]
+        tok_at = pl.ds(pl.multiple_of(i * steps, steps), steps)
+        cvec_ref[tok_at, :] = jnp.full((steps, heads), arrive[requests + i], jnp.int32)
         return carry
 
     lax.fori_loop(0, requests, previous, 0, unroll=4)
@@ -409,17 +411,16 @@
     lax.fori_loop(0, requests, lambda i, c: (save_state(i).wait(), c)[1], 0)
 
 
-def final_kernel(slot_ref, len_ref, recv_ref, out_ref, order, *, heads_dev, inner_all):
+def final_kernel(info, recv_ref, out_ref, order, *, heads_dev, inner_all):
     requests, steps, part = out_ref.shape
     peers = requests // 2
     pair = 2 * steps
     data_rows = 2 * pair
-    base = lax.axis_index("req") * requests
 
     def note(i, owner, j):
         order[owner * 2 + j] = i
 
-    visit(slot_ref, base, requests, note)
+    visit(info, 0, requests, note)
     groups = data_rows // STAT_ROWS
     view = recv_ref.reshape(peers, heads_dev, groups + 1, STAT_ROWS, 128)
     own = lax.broadcasted_iota(jnp.int32, (pair, 128), 0) == lax.broadcasted_iota(
@@ -439,7 +440,7 @@
         scale = lax.rsqrt(total / inner_all + 1e-05)
         for j in range(2):
             i = order[o * 2 + j]
-            keep = place < len_ref[base + i]
+            keep = place < info[requests + i]
             for half in range(2):
                 at = half * pair + j * steps
                 value = acc[at : at + steps, :] * scale[j * steps : (j + 1) * steps, :]
@@ -524,7 +525,6 @@
     rows = (both // (2 * steps)) % requests
     counts = both % (2 * steps)
     arrive = jnp.concatenate([rows, counts])
-    count_col = jnp.broadcast_to(counts[:, None, None], (requests, steps, heads)).reshape(tokens, heads)
 
     states = in_hbm(ssm_state.reshape(requests, inner, nstate))
     turned = pl.pallas_call(
@@ -552,7 +552,7 @@
             pltpu.HBM((requests, steps, inner), bf16),
             pltpu.HBM((requests, steps, bc_cols), bf16),
         ),
-        in_specs=[smem()] + vmem(11) + hbm(4),
+        in_specs=[smem()] + vmem(10) + hbm(4),
         out_specs=tuple(hbm(6)),
         scratch_shapes=[
             pltpu.VMEM((requests, 8 + steps, inner), f32),
@@ -573,6 +573,7 @@
             pltpu.VMEM((inner, width), bf16),
             pltpu.VMEM((requests, nstate, inner), bf16),
             pltpu.VMEM((requests, 1, heads), f32),
+            pltpu.VMEM((tokens, heads), jnp.int32),
             pltpu.SemaphoreType.DMA((heads_dev,)),
             pltpu.SemaphoreType.DMA((5,)),
             pltpu.SemaphoreType.DMA((5,)),
@@ -590,7 +591,6 @@
         a_log[None, :],
         jnp.repeat(d_skip, headdim)[None, :],
         norm_gain[None, :],
-        count_col,
         conv_x_state,
         conv_bc_state,
         in_hbm(w_zx.reshape(width, 2 * inner)),
@@ -620,15 +620,21 @@
         cost_estimate=pl.CostEstimate(flops=2 * 10**9, bytes_accessed=20 * MIB, transcendentals=0),
         name="update",
     )(arrive, push, b_conv, decay, x_in, bc_in, conv_x_state, conv_bc_state, states)
+    mine = jnp.concatenate(
+        [
+            lax.dynamic_slice_in_dim(slot, me * requests, requests),
+            lax.dynamic_slice_in_dim(lengths, me * requests, requests),
+        ]
+    )
     out = pl.pallas_call(
         functools.partial(final_kernel, heads_dev=heads_dev, inner_all=inner * heads_dev),
         out_shape=jax.ShapeDtypeStruct((requests, steps, part), bf16),
-        in_specs=[smem(), smem()] + vmem(1),
+        in_specs=[smem()] + vmem(1),
         out_specs=vmem(1)[0],
         scratch_shapes=[pltpu.SMEM((requests,), jnp.int32)],
         compiler_params=pltpu.CompilerParams(vmem_limit_bytes=4 * MIB),
         name="place_rows",
-    )(slot, lengths, returned)
+    )(mine, returned)
     return (out, new_state.reshape(ssm_state.shape), new_conv_x, new_conv_bc)
 
 

time: 94.8 us -> 95.3 us (level)
  waiting for transfers between devices: 32.8 us -> 30.9 us
  local copies, waits for them, and re-layouts: 9.84 us -> 11.6 us
    all_to_all x1, waiting for transfers between devices: 15.7 us -> 13.7 us  [per_device(): lax.all_to_all(leaving, ('req', 'head'), split_axis=0, concat_axis=0, til...]
    dynamic_slice x0 -> x2, local copies, waits for them, and re-layouts: none -> 1.51 us  [the longest x1 0.76 us: per_device(): lax.dynamic_slice_in_dim(lengths, me * requests, requests)]
    unnamed x40 -> x46, local copies, waits for them, and re-layouts: 9.09 us -> 9.66 us
  transfers between devices with their start and end apart: 2 -> 2, of which waited for: 2 -> 2; matrix products, arithmetic and copies ran while one was open for 9% -> 11% of each run, Pallas kernels for 20% -> 20%
where the time goes in v5:
time: 95.3 us; the launch traced here: 94.8 us
  Pallas kernels  34.3 us (36%)
  waiting for transfers between devices  30.9 us (32%)
  starting transfers between devices  16.2 us (17%)
  local copies, waits for them, and re-layouts  11.6 us (12%)
    all_to_all x1, waiting for transfers between devices, per_device(): lax.all_to_all(outgoing, ('req', 'head'), split_axis=0, concat_axis=0, ti...  17.2 us
    all_to_all x1, waiting for transfers between devices, per_device(): lax.all_to_all(leaving, ('req', 'head'), split_axis=0, concat_axis=0, til...  13.7 us
    pallas_call x1, Pallas kernels, per_device(): pl.pallas_call(state_kernel, out_shape=(pltpu.HBM((requests, inner, nstat...  12.8 us
    all_to_all x1, starting transfers between devices, per_device(): lax.all_to_all(outgoing, ('req', 'head'), split_axis=0, concat_axis=0, ti...  11.5 us
    pallas_call x1, Pallas kernels, per_device(): pl.pallas_call(functools.partial(mix_kernel, heads_dev=heads_dev), out_sh...  10.5 us
    unnamed x46, local copies, waits for them, and re-layouts  9.66 us
    pallas_call x1, Pallas kernels, per_device(): pl.pallas_call(stage_kernel, out_shape=pltpu.HBM((requests, nstate, inner...  6.26 us
    all_to_all x1, starting transfers between devices, per_device(): lax.all_to_all(leaving, ('req', 'head'), split_axis=0, concat_axis=0, til...  4.75 us
  transfers between devices with their start and end apart: 2, of which 2 were waited for; matrix products, arithmetic and copies ran while one was open for 11% of the time, Pallas kernels for 20%

profile of v5, /device:TPU:1, one launch (start us, length us, event | category | flops | bytes accessed | tf_op | source)
XLA Modules:
  0.0 94.8 jit_solution(8868771246234669772)
XLA Ops:
  0.6 0.0 copy-start.16
  0.7 2.6 %send_rows.1 = bf16[256,16,256]{2,1,0:T(8,128)(2,1)} custom-call(s32[512]{0:T(512)} %slot_ref.1, bf16[32,16,256]{2,1,0:T(8,128)(2,1)} %hid_ref.1), custom_call_target="tpu_custom_call" | custom-call | tf_op jit(solution)/shard_map/send_rows/pallas_call | solution.py:504
  3.3 11.5 %all-to-all-start = ((bf16[256,16,256]{2,1,0:T(8,128)(2,1)}), bf16[256,16,256]{2,1,0:T(8,128)(2,1)S(1)}, u32[]{:S(2)}, u32[]{:S(2)}) async-start(bf16[256,16,256]{2,1,0:T(8,128)(2,1)} %send_rows.1), calls=%async_computation | async-start | bytes 4194304 | tf_op jit(solution)/shard_map/all_to_all | solution.py:516
  14.8 0.1 reshape.34
  14.9 0.1 broadcast_in_dim.21
  15.0 0.1 broadcast_in_dim_reshape.3.skip_ref
  15.1 0.1 reshape.35
  15.1 0.1 select_reduce_fusion.1
  15.3 0.1 copy.37
  15.4 0.1 reshape.36
  15.5 0.1 copy.40.cb_ref
  15.6 0.1 copy.39.cx_ref
  15.7 0.3 copy.38.wdt_ref
  16.0 5.4 %copy.45 = bf16[256,8,2,512]{3,1,2,0:T(8,128)(2,1)} copy(bf16[256,8,2,512]{3,2,1,0:T(2,128)(2,1)} %bitcast.15) | data formatting | bytes 8388608
  21.4 0.1 pad_add_fusion.2.arrive
  21.5 0.0 copy-start.12
  21.5 6.3 %stage.1.turned_hbm = bf16[32,128,512]{2,1,0:T(8,128)(2,1)} custom-call(s32[64]{0:T(128)S(1)} %pad_add_fusion.2.arrive, f32[32,512,128]{2,1,0:T(8,128)} %bitcast.13), custom_call_target="tpu_custom_call" | custom-call | flops 1000000000 | bytes 20971520 | tf_op jit(solution)/shard_map/stage/pallas_call | solution.py:530
  27.8 17.2 %all-to-all-done.recv_ref = bf16[256,16,256]{2,1,0:T(8,128)(2,1)S(1)} async-done(((bf16[256,16,256]{2,1,0:T(8,128)(2,1)}), bf16[256,16,256]{2,1,0:T(8,128)(2,1)S(1)}, u32[]{:S(2)}, u32[]{:S(2)}) %all-to-all-start) | async-done | bytes 2097184 | tf_op jit(solution)/shard_map/all_to_all | solution.py:516
  45.0 10.5 %mix.1 = (bf16[16,8,17,4,128]{4,3,2,1,0:T(4,128)(2,1)}, bf16[32,16,512]{2,1,0:T(8,128)(2,1)}, bf16[32,16,128]{2,1,0:T(8,128)(2,1)}, f32[32,1,8]{2,1,0:T(1,128)},...) custom-call(s32[64]{0:T(128)S(1)} %pad_add_fusion.2.arrive, bf16[256,16,256]{2,1,0:T(8,128)(2,1)S(1)} %all-to-all-done.recv_ref, ...), custom_call_target="tpu_custom_call" | custom-call | flops 4000000000 | bytes 8388608 | tf_op jit(solution)/shard_map/mix/pallas_call | solution.py:545
  55.6 0.0 copy-start.4
  55.6 4.7 %all-to-all-start.1 = ((bf16[128,17,4,128]{3,2,1,0:T(4,128)(2,1)}), bf16[128,17,4,128]{3,2,1,0:T(4,128)(2,1)S(1)}, u32[]{:S(2)}, u32[]{:S(2)}) async-start(bf16[128,17,4,128]{3,2,1,0:T(4,128)(2,1)} %bitcast.17), calls=%async_computation.1 | async-start | bytes 4456448 | tf_op jit(solution)/shard_map/all_to_all | solution.py:602
  60.4 0.8 dynamic_slice.7
  61.1 0.8 dynamic_slice.6
  61.9 0.6 pad_add_fusion.1.info
  62.5 1.0 %copy-done.1 = bf16[32,16,512]{2,1,0:T(8,128)(2,1)S(1)} copy-done((bf16[32,16,512]{2,1,0:T(8,128)(2,1)S(1)}, bf16[32,16,512]{2,1,0:T(8,128)(2,1)}, u32[]{:S(2)}) %copy-start.1) | copy-done | bytes 524312
  63.6 0.6 copy-done.6
  64.2 12.8 %update.1 = (f32[32,512,128]{2,1,0:T(8,128)}, f32[32,3,512]{2,1,0:T(4,128)S(1)}, f32[32,3,256]{2,1,0:T(4,128)S(1)}) custom-call(s32[64]{0:T(128)S(1)} %copy-done.6, bf16[32,16,512]{2,1,0:T(8,128)(2,1)S(1)} %copy-done, bf16[32,16,128]{2,1,0:T(8,128)(2,1)S(1)} %copy-done.3, f32[32,1,8]{2,1,0:T(1,128)S(1)} %copy-done.4, bf16[32,16,512]{2,1,0:T(8,128)(2,1)S(1)} %copy-done.1, ...), custom_call_target="tpu_custom_call" | custom-call | flops 2000000000 | bytes 20971520 | tf_op jit(solution)/shard_map/update/pallas_call | solution.py:603
  77.0 0.7 copy.44
  77.6 0.7 copy.43
  78.4 13.7 %all-to-all-done.1.recv_ref = bf16[128,17,4,128]{3,2,1,0:T(4,128)(2,1)S(1)} async-done(((bf16[128,17,4,128]{3,2,1,0:T(4,128)(2,1)}), bf16[128,17,4,128]{3,2,1,0:T(4,128)(2,1)S(1)}, u32[]{:S(2)}, u32[]{:S(2)}) %all-to-all-start.1) | async-done | bytes 2228256 | tf_op jit(solution)/shard_map/all_to_all | solution.py:602
  92.1 0.6 copy-done.7
  92.7 2.1 %place_rows.1 = bf16[32,16,256]{2,1,0:T(8,128)(2,1)} custom-call(s32[64]{0:T(128)S(1)} %copy-done.7, bf16[128,17,4,128]{3,2,1,0:T(4,128)(2,1)S(1)} %all-to-all-done.1.recv_ref), custom_call_target="tpu_custom_call" | custom-call | tf_op jit(solution)/shard_map/place_rows/pallas_call | solution.py:629
  (38 shorter events, 0.1 us)
Async XLA Ops:
  0.6 14.2 %copy-start.16 = (s32[512]{0:T(512)S(1)}, s32[512]{0:T(512)}, u32[]{:S(2)}) copy-start(s32[512]{0:T(512)} %slot_ref.1) | copy-start | bytes 6148
  0.6 14.3 %copy-start.19 = (f32[8]{0:T(128)S(1)}, f32[8]{0:T(128)}, u32[]{:S(2)}) copy-start(f32[8]{0:T(128)} %param.25) | copy-start | bytes 100
  0.7 14.4 %copy-start.18 = (s32[512]{0:T(512)S(1)}, s32[512]{0:T(512)}, u32[]{:S(2)}) copy-start(s32[512]{0:T(512)} %param.32) | copy-start | bytes 6148
  0.7 14.4 %copy-start.17 = (s32[512]{0:T(512)S(1)}, s32[512]{0:T(512)}, u32[]{:S(2)}) copy-start(s32[512]{0:T(512)} %param.33) | copy-start | bytes 6148
  0.7 14.8 %copy-start.14 = (f32[32,3,256]{2,0,1:T(8,128)S(1)}, f32[32,3,256]{2,0,1:T(8,128)}, u32[]{:S(2)}) copy-start(f32[32,3,256]{2,0,1:T(8,128)} %param.30) | copy-start | bytes 294916
  0.7 14.9 %copy-start.13 = (f32[32,3,512]{2,0,1:T(8,128)S(1)}, f32[32,3,512]{2,0,1:T(8,128)}, u32[]{:S(2)}) copy-start(f32[32,3,512]{2,0,1:T(8,128)} %param.29) | copy-start | bytes 589828
  0.7 15.0 %copy-start.15 = (bf16[2048,8]{0,1:T(8,128)(2,1)S(1)}, bf16[2048,8]{0,1:T(8,128)(2,1)}, u32[]{:S(2)}) copy-start(bf16[2048,8]{0,1:T(8,128)(2,1)} %param.20) | copy-start | bytes 98308
  3.3 41.6 %all-to-all-start = ((bf16[256,16,256]{2,1,0:T(8,128)(2,1)}), bf16[256,16,256]{2,1,0:T(8,128)(2,1)S(1)}, u32[]{:S(2)}, u32[]{:S(2)}) async-start(bf16[256,16,256]{2,1,0:T(8,128)(2,1)} %send_rows.1), calls=%async_computation | async-start | bytes 4194304 | tf_op jit(solution)/shard_map/all_to_all | solution.py:516
  21.5 23.5 %copy-start.5 = (s32[64]{0:T(128)}, s32[64]{0:T(128)S(1)}, u32[]{:S(2)}) copy-start(s32[64]{0:T(128)S(1)} %pad_add_fusion.2.arrive) | copy-start | bytes 772
  21.5 23.5 %copy-start.8 = (f32[5,512]{1,0:T(8,128)S(1)}, f32[5,512]{1,0:T(8,128)}, u32[]{:S(2)}) copy-start(f32[5,512]{1,0:T(8,128)} %cxw_ref.1) | copy-start | bytes 30724
  21.5 23.5 %copy-start.9 = (f32[5,256]{1,0:T(8,128)S(1)}, f32[5,256]{1,0:T(8,128)}, u32[]{:S(2)}) copy-start(f32[5,256]{1,0:T(8,128)} %cbw_ref.1) | copy-start | bytes 15364
  21.5 23.5 %copy-start.10 = (f32[512]{0:T(512)S(1)}, f32[512]{0:T(512)}, u32[]{:S(2)}) copy-start(f32[512]{0:T(512)} %param.26) | copy-start | bytes 6148
  21.5 23.5 %copy-start.11 = (f32[8]{0:T(128)S(1)}, f32[8]{0:T(128)}, u32[]{:S(2)}) copy-start(f32[8]{0:T(128)} %param.23) | copy-start | bytes 100
  21.5 23.5 %copy-start.12 = (f32[8]{0:T(128)S(1)}, f32[8]{0:T(128)}, u32[]{:S(2)}) copy-start(f32[8]{0:T(128)} %param.24) | copy-start | bytes 100
  55.6 6.9 %copy-start = (bf16[32,16,512]{2,1,0:T(8,128)(2,1)S(1)}, bf16[32,16,512]{2,1,0:T(8,128)(2,1)}, u32[]{:S(2)}) copy-start(bf16[32,16,512]{2,1,0:T(8,128)(2,1)} %get-tuple-element.14.push_ref) | copy-start | bytes 1572868
  55.6 6.9 %copy-start.2 = (bf16[32,16,256]{2,1,0:T(8,128)(2,1)S(1)}, bf16[32,16,256]{2,1,0:T(8,128)(2,1)}, u32[]{:S(2)}) copy-start(bf16[32,16,256]{2,1,0:T(8,128)(2,1)} %get-tuple-element.18.bin_ref) | copy-start | bytes 786436
  55.6 6.9 %copy-start.3 = (bf16[32,16,128]{2,1,0:T(8,128)(2,1)S(1)}, bf16[32,16,128]{2,1,0:T(8,128)(2,1)}, u32[]{:S(2)}) copy-start(bf16[32,16,128]{2,1,0:T(8,128)(2,1)} %get-tuple-element.15.b_ref) | copy-start | bytes 393220
  55.6 6.9 %copy-start.4 = (f32[32,1,8]{2,1,0:T(1,128)S(1)}, f32[32,1,8]{2,1,0:T(1,128)}, u32[]{:S(2)}) copy-start(f32[32,1,8]{2,1,0:T(1,128)} %get-tuple-element.16.dec_ref) | copy-start | bytes 3076
  55.6 36.5 %all-to-all-start.1 = ((bf16[128,17,4,128]{3,2,1,0:T(4,128)(2,1)}), bf16[128,17,4,128]{3,2,1,0:T(4,128)(2,1)S(1)}, u32[]{:S(2)}, u32[]{:S(2)}) async-start(bf16[128,17,4,128]{3,2,1,0:T(4,128)(2,1)} %bitcast.17), calls=%async_computation.1 | async-start | bytes 4456448 | tf_op jit(solution)/shard_map/all_to_all | solution.py:602
  62.5 1.0 %copy-start.1 = (bf16[32,16,512]{2,1,0:T(8,128)(2,1)S(1)}, bf16[32,16,512]{2,1,0:T(8,128)(2,1)}, u32[]{:S(2)}) copy-start(bf16[32,16,512]{2,1,0:T(8,128)(2,1)} %get-tuple-element.17.xin_ref) | copy-start | bytes 1572868
  63.6 0.6 copy-start.6
  92.1 0.6 copy-start.7
